TPU v7x, 512 devices: a whole 4x8x8 slice. The times are simulated.
512 devices in a mesh: dp: 32 (over z, x_lo, core), seq: 16 (over y, x_hi).
Axes of the slice: x: 4 (x_hi: 2, x_lo: 2; x = x_hi * 2 + x_lo), y: 8, z: 8, core: 2. Of those that a mesh axis runs over, the one named last changes fastest.
Arguments:
- query_in: bfloat16 [32, 2048, 2048], P('dp', 'seq'), may hold values from -6 to 6
- key_in: bfloat16 [32, 2048, 2048], P('dp', 'seq'), may hold values from -6 to 6
- value_in: bfloat16 [32, 2048, 2048], P('dp', 'seq'), may hold values from -6 to 6
- grad_out: bfloat16 [32, 2048, 2048], P('dp', 'seq'), may hold values from -6 to 6
- w_query: bfloat16 [2048, 128], replicated, may hold values from -0.5 to 0.5
- w_key: bfloat16 [2048, 128], replicated, may hold values from -0.5 to 0.5
- norm_gain: float32 [2048], replicated, may hold values from 0.1 to 1.9
Outputs:
- grad_query: bfloat16 [32, 2048, 2048], P('dp', 'seq')
- grad_key: bfloat16 [32, 2048, 2048], P('dp', 'seq')
- grad_value: bfloat16 [32, 2048, 2048], P('dp', 'seq')
- grad_w_query: float32 [2048, 128], P('dp')
- grad_w_key: float32 [2048, 128], P('dp')
- grad_gain: float32 [2048], P('dp')
All inputs are finite; a program needn't handle non-finite values.
Results may differ from a plain program's by a relative error of at most 0.0077.
Values sent between devices are 32-bit elements; how exact they have to be, the bound alone decides.
A program may use at most 128 MiB of HBM per device.

v0:
```python
import jax
import jax.numpy as jnp
from jax import lax
from jax.sharding import PartitionSpec as P

HEAD = 128


norm_eps = 1e-05
highest = lax.Precision.HIGHEST


def entering(value, axis, combine, identity, reverse):
    peers, mine = (lax.axis_size(axis), lax.axis_index(axis))
    everything = lax.all_gather(value, axis)
    start = jnp.broadcast_to(jnp.asarray(identity, value.dtype), value.shape)

    def turn(k, before):
        at = peers - 1 - k if reverse else k
        reached = at > mine if reverse else at < mine
        new = combine(before, everything[at])
        return jnp.where(reached, new, before)

    return lax.fori_loop(0, peers, turn, start)


def add_states(earlier, later):
    return earlier + later


def per_device(query_in, key_in, value_in, grad_out, w_query, w_key, norm_gain):
    seq_count, tok_rows, width_all = query_in.shape
    head_count = width_all // HEAD

    def split_heads(tensor):
        return tensor.reshape(seq_count, tok_rows, head_count, HEAD)

    query_h = split_heads(query_in)
    key_h = split_heads(key_in)
    value_h = split_heads(value_in)
    grad_h = split_heads(grad_out)
    map_query = w_query.reshape(head_count, HEAD, HEAD)
    map_key = w_key.reshape(head_count, HEAD, HEAD)
    pre_query = jnp.einsum("bthd,hde->bthe", query_h, map_query, preferred_element_type=jnp.float32)
    pre_key = jnp.einsum("bthd,hde->bthe", key_h, map_key, preferred_element_type=jnp.float32)
    feat_query = (jax.nn.elu(pre_query) + 1.0).astype(jnp.bfloat16)
    feat_key = (jax.nn.elu(pre_key) + 1.0).astype(jnp.bfloat16)
    position = lax.broadcasted_iota(jnp.int32, (tok_rows, tok_rows), 0)
    column = lax.broadcasted_iota(jnp.int32, (tok_rows, tok_rows), 1)
    causal = position >= column
    local_state = jnp.einsum(
        "bthf,bthe->bhfe", feat_key, value_h, preferred_element_type=jnp.float32
    )
    zero_state = jnp.zeros_like(local_state)
    scores = jnp.einsum("bthf,bshf->bhts", feat_query, feat_key, preferred_element_type=jnp.float32)
    attn_weights = jnp.where(causal, scores, 0.0).astype(jnp.bfloat16)
    inner_sum = jnp.einsum(
        "bhts,bshe->bthe", attn_weights, value_h, preferred_element_type=jnp.float32
    )
    prior_state = entering(local_state, "seq", add_states, zero_state, False)
    query_wide = feat_query.astype(jnp.float32)
    numerator = inner_sum + jnp.einsum(
        "bthf,bhfe->bthe", query_wide, prior_state, precision=highest
    )
    inv_rms = lax.rsqrt(jnp.mean(numerator * numerator, axis=-1, keepdims=True) + norm_eps)
    normed = numerator * inv_rms
    gain_h = norm_gain.reshape(head_count, HEAD)
    grad_f = grad_h.astype(jnp.float32)
    grad_normed = grad_f * gain_h
    grad_numer = inv_rms * (
        grad_normed - normed * jnp.mean(grad_normed * normed, axis=-1, keepdims=True)
    )
    grad_gain = jnp.sum(normed * grad_f, axis=(0, 1)).reshape(width_all)
    numer_low = grad_numer.astype(jnp.bfloat16)
    local_adjoint = jnp.einsum(
        "bthf,bthe->bhfe", feat_query, numer_low, preferred_element_type=jnp.float32
    )
    mixed = jnp.einsum("bthe,bshe->bhts", numer_low, value_h, preferred_element_type=jnp.float32)
    mixed_low = jnp.where(causal, mixed, 0.0).astype(jnp.bfloat16)
    grad_fq = jnp.einsum("bhts,bshf->bthf", mixed_low, feat_key, preferred_element_type=jnp.float32)
    grad_fq = grad_fq + jnp.einsum("bthe,bhfe->bthf", grad_numer, prior_state, precision=highest)
    slope_query = jnp.minimum(jnp.exp(pre_query), 1.0)
    pre_grad_q = (grad_fq * slope_query).astype(jnp.bfloat16)
    grad_query = jnp.einsum(
        "bthe,hde->bthd", pre_grad_q, map_query, preferred_element_type=jnp.float32
    )
    sum_wq = jnp.einsum("bthd,bthe->hde", query_h, pre_grad_q, preferred_element_type=jnp.float32)
    later_state = entering(local_adjoint, "seq", add_states, zero_state, True)
    grad_fk = jnp.einsum(
        "bhts,bthf->bshf", mixed_low, feat_query, preferred_element_type=jnp.float32
    )
    grad_fk = grad_fk + jnp.einsum(
        "bshe,bhfe->bshf", value_h.astype(jnp.float32), later_state, precision=highest
    )
    grad_v = jnp.einsum(
        "bhts,bthe->bshe", attn_weights, numer_low, preferred_element_type=jnp.float32
    )
    grad_v = grad_v + jnp.einsum(
        "bshf,bhfe->bshe", feat_key.astype(jnp.float32), later_state, precision=highest
    )
    slope_key = jnp.minimum(jnp.exp(pre_key), 1.0)
    pre_grad_k = (grad_fk * slope_key).astype(jnp.bfloat16)
    grad_key = jnp.einsum("bthe,hde->bthd", pre_grad_k, map_key, preferred_element_type=jnp.float32)
    sum_wk = jnp.einsum("bthd,bthe->hde", key_h, pre_grad_k, preferred_element_type=jnp.float32)
    sum_wq = sum_wq.reshape(width_all, HEAD)
    sum_wk = sum_wk.reshape(width_all, HEAD)
    owned = (
        lax.psum_scatter(sum_wq, "dp", scatter_dimension=0, tiled=True),
        lax.psum_scatter(sum_wk, "dp", scatter_dimension=0, tiled=True),
        lax.psum_scatter(grad_gain, "dp", scatter_dimension=0, tiled=True),
    )
    total_wq, total_wk, total_gain = lax.psum((owned[0], owned[1], owned[2]), "seq")
    out_shape = (seq_count, tok_rows, width_all)
    return (
        grad_query.astype(jnp.bfloat16).reshape(out_shape),
        grad_key.astype(jnp.bfloat16).reshape(out_shape),
        grad_v.astype(jnp.bfloat16).reshape(out_shape),
        total_wq,
        total_wk,
        total_gain,
    )


def solution(mesh):
    in_specs = (
        P("dp", "seq", None),
        P("dp", "seq", None),
        P("dp", "seq", None),
        P("dp", "seq", None),
        P(),
        P(),
        P(),
    )
    out_specs = (
        P("dp", "seq", None),
        P("dp", "seq", None),
        P("dp", "seq", None),
        P("dp", None),
        P("dp", None),
        P("dp"),
    )
    return jax.shard_map(
        per_device, mesh=mesh, in_specs=in_specs, out_specs=out_specs, check_vma=False
    )
```

profile of v0, /device:TPU:6, one launch (start us, length us, event | category | flops | bytes accessed | tf_op | source)
XLA Modules:
  0.0 920.4 jit_solution(10773321311588541882)
XLA Ops:
  7.2 1.4 copy.87
  8.6 1.5 copy.86
  10.1 1.3 copy.88
  11.9 1.8 convolution_bitcast_fusion.2
  16.3 1.3 fusion.33
  17.8 1.2 copy.53
  19.0 1.8 fusion.6
  21.6 2.5 convolution_bitcast_fusion
  24.1 226.9 %all-gather.5.cloned.1.call-done = f32[256,128,128]{2,1,0:T(8,128)} async-done(((f32[16,128,128]{2,1,0:T(8,128)}), f32[256,128,128]{2,1,0:T(8,128)}) %all-gather.5.cloned.1.call-update) | async-done | bytes 16777232 | tf_op jit(solution)/shard_map/all_gather | solution.py:15
  251.0 25.8 %while.30 = (s32[]{:T(128)}, f32[1,16,128,128]{3,2,1,0:T(8,128)S(1)}, s32[]{:T(128)}, f32[16,1,16,128,128]{4,3,2,1,0:T(8,128)}, s32[]{:T(128)}, /*index=5*/s32[]{:T(128)}) while((s32[]{:T(128)}, f32[1,16,128,128]{3,2,1,0:T(8,128)S(1)}, s32[]{:T(128)}, f32[16,1,16,128,128]{4,3,2,1,0:T(8,128)}, s32[]{:T(128)}, ...), condition=%wide.region_1.2_spmd.clone, body=%wide.region_0.1_spmd.clone.sunk | while | flops 786436 | bytes 3145829 | solution.py:24
  251.0 1.6 add_select_fusion.4
  252.6 1.6 add_select_fusion.4
  254.2 1.6 add_select_fusion.4
  255.9 1.6 add_select_fusion.4
  257.5 1.6 add_select_fusion.4
  259.1 1.6 add_select_fusion.4
  260.7 1.6 add_select_fusion.4
  262.3 1.6 add_select_fusion.4
  263.9 1.6 add_select_fusion.4
  265.5 1.6 add_select_fusion.4
  267.2 1.6 add_select_fusion.4
  268.8 1.6 add_select_fusion.4
  270.4 1.6 add_select_fusion.4
  272.0 1.6 add_select_fusion.4
  273.6 1.6 add_select_fusion.4
  275.2 1.6 add_select_fusion.4
  276.8 2.3 multiply_reduce_fusion.2
  281.3 1.5 fusion.27
  282.9 1.7 fusion.7
  284.6 1.5 fusion.36
  286.1 1.3 fusion.37
  287.4 3.3 fusion.10
  291.6 2.6 fusion.38
  294.3 216.0 %all-gather.7.cloned.1.call-done = f32[256,128,128]{2,1,0:T(8,128)} async-done(((f32[16,128,128]{2,1,0:T(8,128)}), f32[256,128,128]{2,1,0:T(8,128)}) %all-gather.7.cloned.1.call-update) | async-done | bytes 16777232 | tf_op jit(solution)/shard_map/all_gather | solution.py:15
  510.4 25.9 %while.31 = (s32[]{:T(128)}, f32[1,16,128,128]{3,2,1,0:T(8,128)S(1)}, s32[]{:T(128)}, f32[16,1,16,128,128]{4,3,2,1,0:T(8,128)}, s32[]{:T(128)}, /*index=5*/s32[]{:T(128)}, s32[]{:T(128)}, s32[]{:T(128)}) while((s32[]{:T(128)}, f32[1,16,128,128]{3,2,1,0:T(8,128)S(1)}, s32[]{:T(128)}, f32[16,1,16,128,128]{4,3,2,1,0:T(8,128)}, ...), condition=%wide.region_5.6_spmd.clone, body=%wide.region_4.5_spmd.clone.sunk | while | flops 786440 | bytes 3145891 | solution.py:24
  510.4 1.6 add_select_fusion.5
  512.0 1.6 add_select_fusion.5
  513.6 1.6 add_select_fusion.5
  515.2 1.6 add_select_fusion.5
  516.8 1.6 add_select_fusion.5
  518.4 1.6 add_select_fusion.5
  520.1 1.6 add_select_fusion.5
  521.7 1.6 add_select_fusion.5
  523.3 1.6 add_select_fusion.5
  524.9 1.6 add_select_fusion.5
  526.5 1.6 add_select_fusion.5
  528.2 1.6 add_select_fusion.5
  529.8 1.6 add_select_fusion.5
  531.4 1.6 add_select_fusion.5
  533.0 1.6 add_select_fusion.5
  534.7 1.6 add_select_fusion.5
  536.3 2.7 fusion.11
  539.7 2.5 fusion.39
  542.3 1.3 dynamic-slice
  544.3 1.3 convolution_convert_fusion.1
  546.6 54.3 %all-reduce = f32[2048]{0:T(1024)S(1)} all-reduce(f32[2048]{0:T(1024)S(1)} %bitcast.164), channel_id=6, replica_groups=mesh['dp'=32,'seq'=16] {'dp'}, use_global_device_ids=true, to_apply=%region_11.12.clone | all-reduce | flops 2048 | bytes 16384
  601.5 1.5 fusion.25
  604.0 24.3 %reduce-scatter.3.cloned.1.call-done = f32[64,128]{1,0:T(8,128)} async-done(((f32[2048,128]{1,0:T(8,128)}), f32[64,128]{1,0:T(8,128)}) %reduce-scatter.3.cloned.1.call-update) | async-done | bytes 32784 | tf_op jit(solution)/shard_map/reduce_scatter | solution.py:108
  628.3 120.3 %reduce-scatter.5.cloned.1.call-done = f32[64,128]{1,0:T(8,128)} async-done(((f32[2048,128]{1,0:T(8,128)}), f32[64,128]{1,0:T(8,128)}) %reduce-scatter.5.cloned.1.call-update) | async-done | bytes 32784 | tf_op jit(solution)/shard_map/reduce_scatter | solution.py:109
  748.6 1.5 convolution_convert_fusion
  752.1 157.9 %all-reduce.4.cloned.1.call-done = (f32[64,128]{1,0:T(8,128)}, f32[64,128]{1,0:T(8,128)}, f32[64]{0:T(128)}) async-done(((f32[64,128]{1,0:T(8,128)}, f32[64,128]{1,0:T(8,128)}, f32[64]{0:T(128)}), (f32[64,128]{1,0:T(8,128)}, f32[64,128]{1,0:T(8,128)}, f32[64]{0:T(128)})) %all-reduce.4.cloned.1.call-update) | async-done | bytes 65808 | tf_op jit(solution)/shard_map/psum | solution.py:112
  910.1 1.4 copy.112
  911.4 1.4 copy.113
  912.8 1.1 copy.114
  (56 shorter events, 12.5 us)
Async XLA Ops:
  7.2 4.3 copy-start
  7.2 243.8 %all-gather.5.cloned.1.call-start = ((), (), s32[]{:S(2)}) async-start(), calls=%async_computation.4 | async-start | bytes 17825792 | tf_op jit(solution)/shard_map/all_gather | solution.py:15
  8.6 9.1 copy-start.12
  10.1 7.6 copy-start.11
  11.5 4.1 copy-start.8
  11.8 3.7 copy-start.7
  11.9 267.3 %copy-start.15 = (f32[2048]{0:T(1024)S(1)}, f32[2048]{0:T(1024)}, u32[]{:S(2)}) copy-start(f32[2048]{0:T(1024)} %param.17) | copy-start | bytes 24580
  13.6 1.0 copy-start.5
  15.5 0.8 copy-start.3
  17.7 492.7 %all-gather.7.cloned.1.call-start = ((), (), s32[]{:S(2)}) async-start(), calls=%async_computation.5 | async-start | bytes 17825792 | tf_op jit(solution)/shard_map/all_gather | solution.py:15
  19.0 263.9 %copy-start.2 = (f32[1,128,2048]{1,2,0:T(8,128)}, f32[1,128,2048]{1,2,0:T(8,128)S(1)}, u32[]{:S(2)}) copy-start(f32[1,128,2048]{1,2,0:T(8,128)S(1)} %copy.53) | copy-start | bytes 3145732
  20.8 0.8 copy-start.9
  279.1 1.0 copy-start.1
  280.5 0.8 copy-start.10
  282.8 345.5 %reduce-scatter.3.cloned.1.call-start = ((), (), s32[]{:S(2)}) async-start(), calls=%async_computation.2 | async-start | bytes 1081344 | tf_op jit(solution)/shard_map/reduce_scatter | solution.py:108
  290.8 0.8 copy-start.13
  291.6 244.7 %copy-start.6 = (f32[1,128,16,128]{1,3,2,0:T(8,128)S(1)}, f32[1,128,16,128]{1,3,2,0:T(8,128)}, u32[]{:S(2)}) copy-start(f32[1,128,16,128]{1,3,2,0:T(8,128)} %copy-done.5) | copy-start | bytes 3145732
  291.6 311.4 %copy-start.4 = (bf16[128,16,128]{0,2,1:T(8,128)(2,1)S(1)}, bf16[128,16,128]{0,2,1:T(8,128)(2,1)}, u32[]{:S(2)}) copy-start(bf16[128,16,128]{0,2,1:T(8,128)(2,1)} %copy-done.3) | copy-start | bytes 1572868
  294.3 454.3 %reduce-scatter.5.cloned.1.call-start = ((), (), s32[]{:S(2)}) async-start(), calls=%async_computation.3 | async-start | bytes 1081344 | tf_op jit(solution)/shard_map/reduce_scatter | solution.py:109
  538.9 0.8 copy-start.14
  542.3 367.8 %all-reduce.4.cloned.1.call-start = ((), (), s32[]{:S(2)}) async-start(), calls=%async_computation.6 | async-start | bytes 132096 | tf_op jit(solution)/shard_map/psum | solution.py:112
Sparse Core Ops, SparseCore 0:
  17.8 233.1 all-gather.4
  282.9 227.3 all-gather.6
  513.1 115.1 reduce-scatter.2
  631.2 117.3 reduce-scatter.4
  752.1 157.8 all-reduce.3
where the time goes:
time: 923 us; the launch traced here: 920 us
  waiting for transfers between devices  746 us (81%)
  blocking collectives  54.3 us (6%)
  other arithmetic  52.9 us (6%)
  matrix products  32.5 us (4%)
  local copies, waits for them, and re-layouts  19.4 us (2%)
  between operations  14.8 us (2%)
    all_gather x2, waiting for transfers between devices, entering(): everything = lax.all_gather(value, axis)  443 us
    psum x1, waiting for transfers between devices, per_device(): lax.psum((owned[0], owned[1], owned[2]), 'seq')  158 us
    reduce_scatter x1, waiting for transfers between devices, per_device(): lax.psum_scatter(sum_wk, 'dp', scatter_dimension=0, tiled=True)  120 us
    unnamed x1, blocking collectives  54.3 us
    select_n x32, other arithmetic, turn(): return jnp.where(reached, new, before)  50.9 us
    reduce_scatter x1, waiting for transfers between devices, per_device(): lax.psum_scatter(sum_wq, 'dp', scatter_dimension=0, tiled=True)  24.3 us
  transfers between devices with their start and end apart: 5, of which 5 were waited for; matrix products, arithmetic and copies ran while one was open for 6% of the time, Pallas kernels for 0%

commit v1 on v0

--- a/solution.py
+++ b/solution.py
@@ -1,34 +1,244 @@
+import functools
+
 import jax
 import jax.numpy as jnp
 from jax import lax
+from jax.experimental import pallas as pl
+from jax.experimental.pallas import tpu as pltpu
 from jax.sharding import PartitionSpec as P
 
 HEAD = 128
-
+MESH = pl.DeviceIdType.MESH
 
 norm_eps = 1e-05
 highest = lax.Precision.HIGHEST
 
 
-def entering(value, axis, combine, identity, reverse):
-    peers, mine = (lax.axis_size(axis), lax.axis_index(axis))
-    everything = lax.all_gather(value, axis)
-    start = jnp.broadcast_to(jnp.asarray(identity, value.dtype), value.shape)
-
-    def turn(k, before):
-        at = peers - 1 - k if reverse else k
-        reached = at > mine if reverse else at < mine
-        new = combine(before, everything[at])
-        return jnp.where(reached, new, before)
-
-    return lax.fori_loop(0, peers, turn, start)
-
-
-def add_states(earlier, later):
-    return earlier + later
-
-
-def per_device(query_in, key_in, value_in, grad_out, w_query, w_key, norm_gain):
+def scan_kernel(rows, reverse, local, out, peer, inbox, outbox, sx, rx, sy, ry):
+    heads = local.shape[0]
+    dp, seq = lax.axis_index("dp"), lax.axis_index("seq")
+    y, half = seq // 2, seq % 2
+    partner = y * 2 + (1 - half)
+    step = rows - 1 if reverse else 1
+    ahead = ((y + step) % rows) * 2 + half
+    behind = ((y + rows - step) % rows) * 2 + half
+    first, last = (rows - 1, 0) if reverse else (0, rows - 1)
+    barrier = pltpu.get_barrier_semaphore()
+    for other in (partner, ahead, behind):
+        pl.semaphore_signal(barrier, inc=1, device_id=(dp, other), device_id_type=MESH)
+    pl.semaphore_wait(barrier, 3)
+
+    def across(h):
+        return pltpu.make_async_remote_copy(
+            src_ref=local.at[h], dst_ref=peer.at[h], send_sem=sx.at[h], recv_sem=rx.at[h],
+            device_id=(dp, partner), device_id_type=MESH)
+
+    def along(h):
+        return pltpu.make_async_remote_copy(
+            src_ref=outbox.at[h], dst_ref=inbox.at[h], send_sem=sy.at[h], recv_sem=ry.at[h],
+            device_id=(dp, ahead), device_id_type=MESH)
+
+    @pl.loop(0, heads)
+    def _(h):
+        across(h).start()
+
+    @pl.when(y == first)
+    def _():
+        inbox[...] = jnp.zeros_like(inbox)
+
+    pick = jnp.where(half == (0 if reverse else 1), 1.0, 0.0).astype(jnp.float32)
+
+    @pl.loop(0, heads)
+    def _(h):
+        across(h).wait_recv()
+
+        @pl.when(y != first)
+        def _():
+            along(h).wait_recv()
+
+        outbox[h] = inbox[h] + (local[h] + peer[h])
+        out[h] = inbox[h] + pick * peer[h]
+
+        @pl.when(y != last)
+        def _():
+            along(h).start()
+
+    @pl.loop(0, heads)
+    def _(h):
+        across(h).wait_send()
+
+        @pl.when(y != last)
+        def _():
+            along(h).wait_send()
+
+
+def scan_states(state, reverse, rows, name, number):
+    heads = state.shape[0]
+    whole = pltpu.VMEM(state.shape, jnp.float32)
+    dma = pltpu.SemaphoreType.DMA((heads,))
+    return pl.pallas_call(
+        functools.partial(scan_kernel, rows, reverse),
+        out_shape=jax.ShapeDtypeStruct(state.shape, jnp.float32),
+        in_specs=[pl.BlockSpec(memory_space=pltpu.VMEM)],
+        out_specs=pl.BlockSpec(memory_space=pltpu.VMEM),
+        scratch_shapes=[whole, whole, whole, dma, dma, dma, dma],
+        compiler_params=pltpu.CompilerParams(collective_id=number, has_side_effects=True),
+        name=name,
+    )(state)
+
+
+def reduce_kernel(depth, rows, part, out, rcore, summed, rz, block, rlo, slim, ry, mine, rhi, full,
+                  score, kcore, sz, kz, slo, klo, sy, ky, syg, kyg, shi, khi, sg, kg):
+    dp, seq = lax.axis_index("dp"), lax.axis_index("seq")
+    z, low, core = dp // 4, (dp // 2) % 2, dp % 2
+    y, half = seq // 2, seq % 2
+
+    def to_z(k):
+        return (((z + k) % depth) * 4 + low * 2 + core, seq)
+
+    def to_y(k):
+        return (dp, ((y + k) % rows) * 2 + half)
+
+    to_core = (z * 4 + low * 2 + (1 - core), seq)
+    to_low = (z * 4 + (1 - low) * 2 + core, seq)
+    to_half = (dp, y * 2 + (1 - half))
+    barrier = pltpu.get_barrier_semaphore()
+    others = [to_core, to_low, to_half]
+    others += [to_z(k) for k in range(1, depth)] + [to_y(k) for k in range(1, rows)]
+    for other in others:
+        pl.semaphore_signal(barrier, inc=1, device_id=other, device_id_type=MESH)
+    pl.semaphore_wait(barrier, len(others))
+
+    def send(src, dst, s, r, device):
+        return pltpu.make_async_remote_copy(
+            src_ref=src, dst_ref=dst, send_sem=s, recv_sem=r, device_id=device, device_id_type=MESH)
+
+    def core_copy(k):
+        at = (z + k) % depth
+        return send(part.at[1 - core, at], rcore.at[k], score.at[k], kcore.at[k], to_core)
+
+    def z_copy(k):
+        return send(summed.at[k], rz.at[k], sz.at[k], kz.at[k], to_z(k))
+
+    @pl.loop(1, depth + 1)
+    def _(k):
+        core_copy(k % depth).start()
+
+    @pl.loop(1, depth)
+    def _(k):
+        core_copy(k).wait_recv()
+        summed[k] = part[core, (z + k) % depth] + rcore[k]
+        z_copy(k).start()
+
+    core_copy(0).wait_recv()
+    block[...] = part[core, z] + rcore[0]
+
+    @pl.loop(1, depth)
+    def _(k):
+        z_copy(k).wait_recv()
+        block[...] += rz[k]
+
+    low_copy = send(block.at[1 - low], rlo, slo, klo, to_low)
+    low_copy.start()
+    low_copy.wait_recv()
+    slim[...] = block[low] + rlo[...]
+
+    def y_copy(k):
+        at = (y + k) % rows
+        return send(slim.at[pl.ds(2 * at, 2)], ry.at[k, pl.ds(0, 2)], sy.at[k], ky.at[k], to_y(k))
+
+    def gain_copy(k):
+        return send(slim.at[pl.ds(2 * rows, 1)], ry.at[k, pl.ds(2, 1)], syg.at[k], kyg.at[k], to_y(k))
+
+    @pl.loop(1, rows)
+    def _(k):
+        y_copy(k).start()
+        gain_copy(k).start()
+
+    mine[pl.ds(0, 2)] = slim[pl.ds(2 * y, 2)]
+    mine[pl.ds(2, 1)] = slim[pl.ds(2 * rows, 1)]
+
+    @pl.loop(1, rows)
+    def _(k):
+        y_copy(k).wait_recv()
+        gain_copy(k).wait_recv()
+        mine[...] += ry[k]
+
+    half_copy = send(mine, rhi, shi, khi, to_half)
+    half_copy.start()
+    half_copy.wait()
+    mine[...] += rhi[...]
+
+    def gather_copy(k):
+        return send(mine.at[pl.ds(0, 2)], full.at[pl.ds(2 * y, 2)], sg.at[k], kg.at[k], to_y(k))
+
+    @pl.loop(1, rows)
+    def _(k):
+        gather_copy(k).start()
+
+    def arrival(k):
+        at = (y + rows - k) % rows
+        return send(mine.at[pl.ds(0, 2)], full.at[pl.ds(2 * at, 2)], sg.at[k], kg.at[k], to_y(k))
+
+    @pl.loop(1, rows)
+    def _(k):
+        at = (y + rows - k) % rows
+        arrival(k).wait_recv()
+        out[pl.ds(2 * at, 2)] = full[pl.ds(2 * at, 2)]
+
+    out[pl.ds(2 * y, 2)] = mine[pl.ds(0, 2)]
+    out[pl.ds(2 * rows, 1)] = mine[pl.ds(2, 1)]
+
+    core_copy(0).wait_send()
+    low_copy.wait_send()
+
+    @pl.loop(1, depth)
+    def _(k):
+        core_copy(k).wait_send()
+        z_copy(k).wait_send()
+
+    @pl.loop(1, rows)
+    def _(k):
+        y_copy(k).wait_send()
+        gain_copy(k).wait_send()
+        gather_copy(k).wait_send()
+
+
+def reduce_gradients(sum_wq, sum_wk, sum_gain, depth, rows):
+    owners = depth * 4
+    own = sum_wq.shape[0] // owners
+    tiles = own // 8
+    both = jnp.stack(
+        [sum_wq.reshape(owners, tiles, 8, HEAD), sum_wk.reshape(owners, tiles, 8, HEAD)], axis=2)
+    both = both.reshape(owners, 2 * tiles, 8, HEAD)
+    gains = jnp.pad(sum_gain.reshape(owners, 1, 1, own), ((0, 0), (0, 0), (0, 7), (0, HEAD - own)))
+    part = jnp.concatenate([both, gains], axis=1)
+    count = 2 * tiles + 1
+    part = part.reshape(depth, 2, 2, count, 8, HEAD).transpose(2, 0, 1, 3, 4, 5)
+    dma = pltpu.SemaphoreType.DMA
+
+    def f32(*shape):
+        return pltpu.VMEM(shape + (8, HEAD), jnp.float32)
+
+    total = pl.pallas_call(
+        functools.partial(reduce_kernel, depth, rows),
+        out_shape=jax.ShapeDtypeStruct((count, 8, HEAD), jnp.float32),
+        in_specs=[pl.BlockSpec(memory_space=pltpu.VMEM)],
+        out_specs=pl.BlockSpec(memory_space=pltpu.VMEM),
+        scratch_shapes=[
+            f32(depth, 2, count), f32(depth, 2, count), f32(depth, 2, count), f32(2, count), f32(count),
+            f32(count), f32(rows, 3), f32(3), f32(3), f32(count),
+            dma((depth,)), dma((depth,)), dma((depth,)), dma((depth,)), dma, dma,
+            dma((rows,)), dma((rows,)), dma((rows,)), dma((rows,)), dma, dma, dma((rows,)), dma((rows,)),
+        ],
+        compiler_params=pltpu.CompilerParams(collective_id=2, has_side_effects=True),
+        name="reduce_gradients",
+    )(part)
+    pairs = total[: 2 * tiles].reshape(tiles, 2, 8, HEAD)
+    return pairs[:, 0].reshape(own, HEAD), pairs[:, 1].reshape(own, HEAD), total[2 * tiles, 0, :own]
+
+
+def per_device(depth, rows, query_in, key_in, value_in, grad_out, w_query, w_key, norm_gain):
     seq_count, tok_rows, width_all = query_in.shape
     head_count = width_all // HEAD
 
@@ -51,13 +261,12 @@
     local_state = jnp.einsum(
         "bthf,bthe->bhfe", feat_key, value_h, preferred_element_type=jnp.float32
     )
-    zero_state = jnp.zeros_like(local_state)
     scores = jnp.einsum("bthf,bshf->bhts", feat_query, feat_key, preferred_element_type=jnp.float32)
     attn_weights = jnp.where(causal, scores, 0.0).astype(jnp.bfloat16)
     inner_sum = jnp.einsum(
         "bhts,bshe->bthe", attn_weights, value_h, preferred_element_type=jnp.float32
     )
-    prior_state = entering(local_state, "seq", add_states, zero_state, False)
+    prior_state = scan_states(local_state[0], False, rows, "prior_scan", 0)[None]
     query_wide = feat_query.astype(jnp.float32)
     numerator = inner_sum + jnp.einsum(
         "bthf,bhfe->bthe", query_wide, prior_state, precision=highest
@@ -85,7 +294,7 @@
         "bthe,hde->bthd", pre_grad_q, map_query, preferred_element_type=jnp.float32
     )
     sum_wq = jnp.einsum("bthd,bthe->hde", query_h, pre_grad_q, preferred_element_type=jnp.float32)
-    later_state = entering(local_adjoint, "seq", add_states, zero_state, True)
+    later_state = scan_states(local_adjoint[0], True, rows, "later_scan", 1)[None]
     grad_fk = jnp.einsum(
         "bhts,bthf->bshf", mixed_low, feat_query, preferred_element_type=jnp.float32
     )
@@ -104,12 +313,7 @@
     sum_wk = jnp.einsum("bthd,bthe->hde", key_h, pre_grad_k, preferred_element_type=jnp.float32)
     sum_wq = sum_wq.reshape(width_all, HEAD)
     sum_wk = sum_wk.reshape(width_all, HEAD)
-    owned = (
-        lax.psum_scatter(sum_wq, "dp", scatter_dimension=0, tiled=True),
-        lax.psum_scatter(sum_wk, "dp", scatter_dimension=0, tiled=True),
-        lax.psum_scatter(grad_gain, "dp", scatter_dimension=0, tiled=True),
-    )
-    total_wq, total_wk, total_gain = lax.psum((owned[0], owned[1], owned[2]), "seq")
+    total_wq, total_wk, total_gain = reduce_gradients(sum_wq, sum_wk, grad_gain, depth, rows)
     out_shape = (seq_count, tok_rows, width_all)
     return (
         grad_query.astype(jnp.bfloat16).reshape(out_shape),
@@ -122,23 +326,12 @@
 
 
 def solution(mesh):
-    in_specs = (
-        P("dp", "seq", None),
-        P("dp", "seq", None),
-        P("dp", "seq", None),
-        P("dp", "seq", None),
-        P(),
-        P(),
-        P(),
-    )
-    out_specs = (
-        P("dp", "seq", None),
-        P("dp", "seq", None),
-        P("dp", "seq", None),
-        P("dp", None),
-        P("dp", None),
-        P("dp"),
-    )
+    tokens = P("dp", "seq", None)
+    body = functools.partial(per_device, mesh.shape["dp"] // 4, mesh.shape["seq"] // 2)
     return jax.shard_map(
-        per_device, mesh=mesh, in_specs=in_specs, out_specs=out_specs, check_vma=False
-    )
+        body,
+        mesh=mesh,
+        in_specs=(tokens, tokens, tokens, tokens, P(), P(), P()),
+        out_specs=(tokens, tokens, tokens, P("dp", None), P("dp", None), P("dp")),
+        check_vma=False,
+    )

time: 923 us -> 208 us (0.23)
  waiting for transfers between devices: 746 us -> 0 us
  Pallas kernels: 0 us -> 164 us
  blocking collectives: 54.3 us -> 0 us
  other arithmetic: 52.9 us -> 3.73 us
  between operations: 14.8 us -> 0.99 us
  matrix products: 32.5 us -> 21.1 us
    all_gather x2 -> x0, waiting for transfers between devices: 443 us -> none  [entering(): everything = lax.all_gather(value, axis)]
    pallas_call x0 -> x3, Pallas kernels: none -> 164 us  [the longest x2 107 us: scan_states(): pl.pallas_call(functools.partial(scan_kernel, rows, reverse), out_shape=j...]
    psum x1 -> x0, waiting for transfers between devices: 158 us -> none  [per_device(): lax.psum((owned[0], owned[1], owned[2]), 'seq')]
    reduce_scatter x2 -> x0, waiting for transfers between devices: 145 us -> none  [the longest x1 120 us: per_device(): lax.psum_scatter(sum_wk, 'dp', scatter_dimension=0, tiled=True)]
    unnamed x1 -> x0, blocking collectives: 54.3 us -> none
    select_n x32 -> x0, other arithmetic: 50.9 us -> none  [turn(): return jnp.where(reached, new, before)]
  transfers between devices with their start and end apart: 5 -> 0, of which waited for: 5 -> 0; matrix products, arithmetic and copies ran while one was open for 6% -> 0% of each run, Pallas kernels for 0% -> 0%
where the time goes in v1:
time: 208 us; the launch traced here: 207 us
  Pallas kernels  164 us (79%)
  matrix products  21.1 us (10%)
  local copies, waits for them, and re-layouts  16.9 us (8%)
  other arithmetic  3.73 us (2%)
    pallas_call x2, Pallas kernels, scan_states(): pl.pallas_call(functools.partial(scan_kernel, rows, reverse), out_shape=j...  107 us
    pallas_call x1, Pallas kernels, reduce_gradients(): pl.pallas_call(functools.partial(reduce_kernel, depth, rows), out_shape=j...  56.6 us
    unnamed x56, local copies, waits for them, and re-layouts  12.3 us

profile of v1, /device:TPU:6, one launch (start us, length us, event | category | flops | bytes accessed | tf_op | source)
XLA Modules:
  0.0 206.7 jit_solution(5292279354296147071)
XLA Ops:
  0.6 0.0 copy-start
  0.6 0.0 copy-start.24
  0.7 1.0 copy-done
  1.7 1.4 copy.87
  3.1 0.0 copy-start.11
  3.1 1.3 convolution_bitcast_fusion.1
  4.4 0.0 copy-done.24
  4.4 0.3 copy.86
  4.7 0.0 copy-start.13
  4.7 0.0 copy-start.3
  4.7 0.0 copy-done.11
  4.7 0.8 copy-done.13
  5.5 0.0 copy-done.19
  5.5 0.3 convolution_bitcast_fusion.2
  5.8 0.2 copy-done.3
  6.1 0.9 fusion.19
  7.0 0.1 copy-done.1
  7.1 0.4 copy-done.23
  7.5 0.2 copy.50
  7.7 0.4 fusion.6
  8.1 0.0 copy-start.7
  8.1 1.3 copy.88
  9.4 0.0 copy-done.7
  9.4 1.5 convolution_bitcast_fusion
  10.9 1.3 fusion.29.local
  12.2 33.4 %prior_scan.1 = f32[16,128,128]{2,1,0:T(8,128)} custom-call(f32[16,128,128]{2,1,0:T(8,128)} %fusion.29.local), custom_call_target="tpu_custom_call" | custom-call | tf_op jit(solution)/shard_map/prior_scan/pallas_call | solution.py:79
  45.6 0.0 copy-start.25
  45.6 2.6 %multiply_reduce_fusion.2 = (f32[128,16]{0,1:T(8,128)S(1)}, f32[1,128,16,128]{1,3,2,0:T(8,128)S(1)}) fusion(f32[16,128,128]{2,1,0:T(8,128)} %convolution_bitcast_fusion, f32[16,128,128]{2,1,0:T(8,128)} %prior_scan.1, bf16[128,16,128]{0,2,1:T(8,128)(2,1)S(1)} %get-tuple-element.24), kind=kOutput, calls=%fused_computation.39 | convolution fusion | flops 403437568 | bytes 3678208 | tf_op jit(solution)/shard_map/bthf,bhfe->bthe/dot_general | solution.py:271
  48.2 0.0 copy-done.25
  48.2 0.7 multiply_reduce_fusion
  49.0 0.4 fusion.31
  49.3 0.0 copy-start.9
  49.3 0.8 copy-done.9
  50.1 0.5 fusion.7
  50.6 0.8 copy-done.21
  51.4 0.5 fusion.32
  51.9 0.0 copy-done.4
  51.9 0.0 copy-done.5
  51.9 1.5 fusion.10
  53.5 0.0 copy-start.15
  53.5 0.8 copy-done.15
  54.3 0.3 convolution_convert_fusion.1
  54.6 1.0 copy.68
  55.6 1.3 fusion.33
  56.9 2.6 %fusion.23.local = f32[16,128,128]{2,1,0:T(8,128)} fusion(bf16[128,16,128]{0,2,1:T(8,128)(2,1)S(1)} %get-tuple-element.24, bf16[1,128,16,128]{1,3,2,0:T(8,128)(2,1)} %copy-done.9), kind=kOutput, calls=%fused_computation.44 | convolution fusion | flops 67108864 | bytes 2097152 | tf_op jit(solution)/shard_map/bthf,bthe->bhfe/dot_general | solution.py:284
  59.4 74.0 %later_scan.1 = f32[16,128,128]{2,1,0:T(8,128)} custom-call(f32[16,128,128]{2,1,0:T(8,128)} %fusion.23.local), custom_call_target="tpu_custom_call" | custom-call | tf_op jit(solution)/shard_map/later_scan/pallas_call | solution.py:79
  133.4 0.0 copy-start.20
  133.4 2.9 %fusion.11 = bf16[128,16,128]{0,2,1:T(8,128)(2,1)S(1)} fusion(f32[16,128,128]{2,1,0:T(8,128)} %fusion.33, f32[16,128,128]{2,1,0:T(8,128)} %later_scan.1, f32[1,128,16,128]{1,3,2,0:T(8,128)S(1)} %copy-done.2, bf16[128,16,128]{2,1,0:T(8,128)(2,1)S(1)} %bitcast.138), kind=kOutput, calls=%fused_computation.28 | convolution fusion | flops 403701760 | bytes 4194304 | tf_op jit(solution)/shard_map/bshe,bhfe->bshf/dot_general | solution.py:301
  136.3 0.8 copy-done.17
  137.1 1.1 convolution_convert_fusion
  138.2 2.0 copy.69
  140.3 0.0 copy-done.10
  140.3 0.3 fusion.21
  140.6 1.8 fusion.5
  142.4 2.1 %copy.70 = bf16[1,128,2048]{2,1,0:T(8,128)(2,1)} copy(bf16[1,128,2048]{1,2,0:T(8,128)(2,1)} %bitcast.149) | data formatting | bytes 1048576
  144.6 0.5 fusion.35
  145.1 0.5 fusion.34
  145.5 0.2 pad_maximum_fusion
  145.7 0.1 reshape_reshape.3
  145.8 1.6 maximum_bitcast_fusion.part
  147.4 56.6 %reduce_gradients.1 = f32[17,8,128]{2,1,0:T(8,128)} custom-call(f32[2,8,2,17,8,128]{5,4,3,2,1,0:T(8,128)} %maximum_bitcast_fusion.part), custom_call_target="tpu_custom_call" | custom-call | tf_op jit(solution)/shard_map/reduce_gradients/pallas_call | solution.py:223
  204.0 0.8 slice.12
  204.9 0.6 slice_bitcast_fusion
  205.5 1.2 slice_bitcast_fusion.2
  (29 shorter events, 0.1 us)
Async XLA Ops:
  0.6 1.0 copy-start
  0.6 3.7 %copy-start.24 = (bf16[1,128,2048]{2,1,0:T(8,128)(2,1)S(1)}, bf16[1,128,2048]{2,1,0:T(8,128)(2,1)}, u32[]{:S(2)}) copy-start(bf16[1,128,2048]{2,1,0:T(8,128)(2,1)} %param.8) | copy-start | bytes 1572868
  1.7 3.8 %copy-start.19 = (bf16[2048,128]{1,0:T(8,128)(2,1)S(1)}, bf16[2048,128]{1,0:T(8,128)(2,1)}, u32[]{:S(2)}) copy-start(bf16[2048,128]{1,0:T(8,128)(2,1)} %param.12) | copy-start | bytes 1572868
  3.1 1.6 copy-start.11
  4.7 0.8 copy-start.13
  4.7 1.4 copy-start.3
  6.1 1.0 copy-start.1
  6.1 1.4 copy-start.23
  8.1 1.4 copy-start.7
  45.6 2.6 %copy-start.25 = (f32[2048]{0:T(1024)S(1)}, f32[2048]{0:T(1024)}, u32[]{:S(2)}) copy-start(f32[2048]{0:T(1024)} %param.13) | copy-start | bytes 24580
  49.3 0.8 copy-start.9
  50.1 1.8 copy-start.4
  50.1 1.8 copy-start.5
  50.6 0.8 copy-start.21
  53.5 0.8 copy-start.15
  54.3 1.3 copy-start.22
  56.9 76.6 %copy-start.2 = (f32[1,128,16,128]{1,3,2,0:T(8,128)S(1)}, f32[1,128,16,128]{1,3,2,0:T(8,128)}, u32[]{:S(2)}) copy-start(f32[1,128,16,128]{1,3,2,0:T(8,128)} %copy-done.1) | copy-start | bytes 3145732
  133.4 3.7 %copy-start.20 = (bf16[2048,128]{1,0:T(8,128)(2,1)S(1)}, bf16[2048,128]{1,0:T(8,128)(2,1)}, u32[]{:S(2)}) copy-start(bf16[2048,128]{1,0:T(8,128)(2,1)} %param.12) | copy-start | bytes 1572868
  136.3 0.8 copy-start.17
  137.1 3.1 %copy-start.8 = (bf16[16,128,128]{2,1,0:T(8,128)(2,1)S(1)}, bf16[16,128,128]{2,1,0:T(8,128)(2,1)}, u32[]{:S(2)}) copy-start(bf16[16,128,128]{2,1,0:T(8,128)(2,1)} %copy-done.7) | copy-start | bytes 1572868
  137.1 3.1 %copy-start.10 = (bf16[1,128,16,128]{1,3,2,0:T(8,128)(2,1)S(1)}, bf16[1,128,16,128]{1,3,2,0:T(8,128)(2,1)}, u32[]{:S(2)}) copy-start(bf16[1,128,16,128]{1,3,2,0:T(8,128)(2,1)} %copy-done.9) | copy-start | bytes 1572868
  137.1 3.4 %copy-start.6 = (f32[16,128,128]{2,1,0:T(8,128)S(1)}, f32[16,128,128]{2,1,0:T(8,128)}, u32[]{:S(2)}) copy-start(f32[16,128,128]{2,1,0:T(8,128)} %later_scan.1) | copy-start | bytes 3145732
  140.6 4.0 %copy-start.14 = (bf16[1,128,2048]{1,2,0:T(8,128)(2,1)S(1)}, bf16[1,128,2048]{1,2,0:T(8,128)(2,1)}, u32[]{:S(2)}) copy-start(bf16[1,128,2048]{1,2,0:T(8,128)(2,1)} %copy-done.13) | copy-start | bytes 1572868
  140.6 4.0 %copy-start.18 = (bf16[128,16,128]{0,2,1:T(8,128)(2,1)S(1)}, bf16[128,16,128]{0,2,1:T(8,128)(2,1)}, u32[]{:S(2)}) copy-start(bf16[128,16,128]{0,2,1:T(8,128)(2,1)} %copy-done.17) | copy-start | bytes 1572868
  142.4 2.6 %copy-start.12 = (bf16[1,128,2048]{1,2,0:T(8,128)(2,1)S(1)}, bf16[1,128,2048]{1,2,0:T(8,128)(2,1)}, u32[]{:S(2)}) copy-start(bf16[1,128,2048]{1,2,0:T(8,128)(2,1)} %copy-done.11) | copy-start | bytes 1572868
  142.4 2.6 %copy-start.16 = (bf16[128,16,128]{0,2,1:T(8,128)(2,1)S(1)}, bf16[128,16,128]{0,2,1:T(8,128)(2,1)}, u32[]{:S(2)}) copy-start(bf16[128,16,128]{0,2,1:T(8,128)(2,1)} %copy-done.15) | copy-start | bytes 1572868

commit v2 on v1

v2 whole, which is shorter than its diff:
```python
import functools

import jax
import jax.numpy as jnp
from jax import lax
from jax.experimental import pallas as pl
from jax.experimental.pallas import tpu as pltpu
from jax.sharding import PartitionSpec as P

HEAD = 128
MESH = pl.DeviceIdType.MESH

norm_eps = 1e-05


def product(left, right, over):
    return lax.dot_general(left, right, ((over[:1], over[1:]), ((), ())), preferred_element_type=jnp.float32)


def two_terms(wide):
    high = wide.astype(jnp.bfloat16)
    return high, (wide - high.astype(jnp.float32)).astype(jnp.bfloat16)


def exchange(src, dst, send_sem, recv_sem, device):
    return pltpu.make_async_remote_copy(
        src_ref=src, dst_ref=dst, send_sem=send_sem, recv_sem=recv_sem, device_id=device, device_id_type=MESH)


def attention_kernel(rows, query, key, value, cotangent, wq, wk, gain, grad_query, grad_key, grad_value, part,
                     local, peer, inbox, outbox, adjoint, peer_adj, inbox_adj, outbox_adj,
                     feat_k, slope_k, part_fk, part_v, sx, rx, sy, ry, sx2, rx2, sy2, ry2):
    heads = local.shape[0]
    dp, seq = lax.axis_index("dp"), lax.axis_index("seq")
    y, half = seq // 2, seq % 2
    top = rows - 1
    partner = (dp, y * 2 + (1 - half))
    above = (dp, ((y + 1) % rows) * 2 + half)
    below = (dp, ((y + rows - 1) % rows) * 2 + half)
    barrier = pltpu.get_barrier_semaphore()
    for other in (partner, above, below):
        pl.semaphore_signal(barrier, inc=1, device_id=other, device_id_type=MESH)
    pl.semaphore_wait(barrier, 3)

    def across(h):
        return exchange(local.at[h], peer.at[h], sx.at[h], rx.at[h], partner)

    def upward(h):
        return exchange(outbox.at[h], inbox.at[h], sy.at[h], ry.at[h], above)

    def across_adj(h):
        return exchange(adjoint.at[h], peer_adj.at[h], sx2.at[h], rx2.at[h], partner)

    def downward(h):
        return exchange(outbox_adj.at[h], inbox_adj.at[h], sy2.at[h], ry2.at[h], below)

    def columns(h):
        return pl.ds(pl.multiple_of(h * HEAD, HEAD), HEAD)

    tokens = query.shape[0]
    position = lax.broadcasted_iota(jnp.int32, (tokens, tokens), 0)
    column = lax.broadcasted_iota(jnp.int32, (tokens, tokens), 1)
    causal = position >= column

    def put_sums(h, which, total):
        own = HEAD // 2
        for core in range(2):
            for tile in range(own // 8):
                start = core * own + tile * 8
                part[core, h // 2, h % 2, 2 * tile + which] = total[start : start + 8]

    @pl.loop(0, heads)
    def _(h):
        at = columns(h)
        pre = product(key[:, at], wk[at, :], (1, 0))
        slope = jnp.exp(jnp.minimum(pre, 0.0))
        feat = jnp.where(pre > 0.0, pre + 1.0, slope).astype(jnp.bfloat16)
        slope_k[h] = slope
        feat_k[h] = feat
        local[h] = product(feat, value[:, at], (0, 0))

        @pl.when(h > 0)
        def _():
            across(h - 1).start()

    @pl.when(y == 0)
    def _():
        inbox[...] = jnp.zeros_like(inbox)

    @pl.when(y == top)
    def _():
        inbox_adj[...] = jnp.zeros_like(inbox_adj)

    across(heads - 1).start()
    is_second = jnp.where(half == 1, 1.0, 0.0).astype(jnp.float32)

    def forward(h):
        at = columns(h)
        fk, v = feat_k[h], value[:, at]
        q, wq_h = query[:, at], wq[at, :]
        pre = product(q, wq_h, (1, 0))
        slope = jnp.exp(jnp.minimum(pre, 0.0))
        fq = jnp.where(pre > 0.0, pre + 1.0, slope).astype(jnp.bfloat16)
        attn = jnp.where(causal, product(fq, fk, (1, 1)), 0.0).astype(jnp.bfloat16)
        inner = product(attn, v, (1, 0))
        across(h).wait_recv()

        @pl.when(y != 0)
        def _():
            upward(h).wait_recv()

        outbox[h] = inbox[h] + (local[h] + peer[h])
        state_high, state_low = two_terms(inbox[h] + is_second * peer[h])

        @pl.when(y != top)
        def _():
            upward(h).start()

        numerator = inner + (product(fq, state_high, (1, 0)) + product(fq, state_low, (1, 0)))
        inv_rms = lax.rsqrt(jnp.mean(numerator * numerator, axis=-1, keepdims=True) + norm_eps)
        normed = numerator * inv_rms
        grad = cotangent[:, at].astype(jnp.float32)
        grad_normed = grad * gain[:, at]
        grad_numer = inv_rms * (
            grad_normed - normed * jnp.mean(grad_normed * normed, axis=-1, keepdims=True))
        low, rest = two_terms(grad_numer)
        adjoint[h] = product(fq, low, (0, 0))
        mixed = jnp.where(causal, product(low, v, (1, 1)), 0.0).astype(jnp.bfloat16)
        grad_fq = product(mixed, fk, (1, 0)) + (
            product(low, state_high, (1, 1)) + (product(low, state_low, (1, 1)) + product(rest, state_high, (1, 1))))
        across_adj(h).start()
        pre_grad = (grad_fq * slope).astype(jnp.bfloat16)
        grad_query[:, at] = product(pre_grad, wq_h, (1, 1)).astype(jnp.bfloat16)
        part_fk[h] = product(mixed, fq, (0, 0))
        part_v[h] = product(attn, low, (0, 0))
        put_sums(h, 0, product(q, pre_grad, (0, 0)))
        gains = jnp.broadcast_to(jnp.sum(normed * grad, axis=0, keepdims=True), (8, HEAD))
        for core in range(2):
            part[core, h // 2, h % 2, HEAD // 8] = gains

    def backward(h):
        at = columns(h)
        across_adj(h).wait_recv()

        @pl.when(y != top)
        def _():
            downward(h).wait_recv()

        outbox_adj[h] = inbox_adj[h] + (adjoint[h] + peer_adj[h])
        state_high, state_low = two_terms(inbox_adj[h] + (1.0 - is_second) * peer_adj[h])

        @pl.when(y != 0)
        def _():
            downward(h).start()

        v, fk, wk_h = value[:, at], feat_k[h], wk[at, :]
        grad_fk = part_fk[h] + (product(v, state_high, (1, 1)) + product(v, state_low, (1, 1)))
        pre_grad = (grad_fk * slope_k[h]).astype(jnp.bfloat16)
        grad_v = part_v[h] + (product(fk, state_high, (1, 0)) + product(fk, state_low, (1, 0)))
        grad_value[:, at] = grad_v.astype(jnp.bfloat16)
        grad_key[:, at] = product(pre_grad, wk_h, (1, 1)).astype(jnp.bfloat16)
        put_sums(h, 1, product(key[:, at], pre_grad, (0, 0)))

    lag = 3 * (top - y)

    @pl.loop(0, heads + 3 * top)
    def _(step):
        @pl.when(step < heads)
        def _():
            forward(step)

        @pl.when(step >= lag)
        def _():
            @pl.when(step < lag + heads)
            def _():
                backward(step - lag)

    @pl.loop(0, heads)
    def _(h):
        across(h).wait_send()
        across_adj(h).wait_send()

        @pl.when(y != top)
        def _():
            upward(h).wait_send()

        @pl.when(y != 0)
        def _():
            downward(h).wait_send()


def attention(query, key, value, cotangent, wq, wk, gain, depth, rows):
    heads = wq.shape[0] // HEAD
    tokens, width = query.shape
    states = pltpu.VMEM((heads, HEAD, HEAD), jnp.float32)
    dma = pltpu.SemaphoreType.DMA((heads,))
    vmem = pl.BlockSpec(memory_space=pltpu.VMEM)
    grads = jax.ShapeDtypeStruct((tokens, width), jnp.bfloat16)
    return pl.pallas_call(
        functools.partial(attention_kernel, rows),
        out_shape=(grads, grads, grads,
                   jax.ShapeDtypeStruct((2, depth, 2, HEAD // 8 + 1, 8, HEAD), jnp.float32)),
        in_specs=[vmem] * 7,
        out_specs=(vmem,) * 4,
        scratch_shapes=[states] * 8
        + [pltpu.VMEM((heads, tokens, HEAD), jnp.bfloat16), pltpu.VMEM((heads, tokens, HEAD), jnp.float32)]
        + [pltpu.VMEM((heads, tokens, HEAD), jnp.float32)] * 2
        + [dma] * 8,
        compiler_params=pltpu.CompilerParams(collective_id=0, has_side_effects=True),
        name="attention",
    )(query, key, value, cotangent, wq, wk, gain)


def reduce_kernel(depth, rows, part, out, rcore, summed, rz, block, rlo, slim, ry, mine, rhi, full,
                  score, kcore, sz, kz, slo, klo, sy, ky, syg, kyg, shi, khi, sg, kg):
    dp, seq = lax.axis_index("dp"), lax.axis_index("seq")
    z, low, core = dp // 4, (dp // 2) % 2, dp % 2
    y, half = seq // 2, seq % 2

    def to_z(k):
        return (((z + k) % depth) * 4 + low * 2 + core, seq)

    def to_y(k):
        return (dp, ((y + k) % rows) * 2 + half)

    to_core = (z * 4 + low * 2 + (1 - core), seq)
    to_low = (z * 4 + (1 - low) * 2 + core, seq)
    to_half = (dp, y * 2 + (1 - half))
    barrier = pltpu.get_barrier_semaphore()
    others = [to_core, to_low, to_half]
    others += [to_z(k) for k in range(1, depth)] + [to_y(k) for k in range(1, rows)]
    for other in others:
        pl.semaphore_signal(barrier, inc=1, device_id=other, device_id_type=MESH)
    pl.semaphore_wait(barrier, len(others))

    def send(src, dst, s, r, device):
        return pltpu.make_async_remote_copy(
            src_ref=src, dst_ref=dst, send_sem=s, recv_sem=r, device_id=device, device_id_type=MESH)

    def core_copy(k):
        at = (z + k) % depth
        return send(part.at[1 - core, at], rcore.at[k], score.at[k], kcore.at[k], to_core)

    def z_copy(k):
        return send(summed.at[k], rz.at[k], sz.at[k], kz.at[k], to_z(k))

    @pl.loop(1, depth + 1)
    def _(k):
        core_copy(k % depth).start()

    @pl.loop(1, depth)
    def _(k):
        core_copy(k).wait_recv()
        summed[k] = part[core, (z + k) % depth] + rcore[k]
        z_copy(k).start()

    core_copy(0).wait_recv()
    block[...] = part[core, z] + rcore[0]

    @pl.loop(1, depth)
    def _(k):
        z_copy(k).wait_recv()
        block[...] += rz[k]

    low_copy = send(block.at[1 - low], rlo, slo, klo, to_low)
    low_copy.start()
    low_copy.wait_recv()
    slim[...] = block[low] + rlo[...]

    def y_copy(k):
        at = (y + k) % rows
        return send(slim.at[pl.ds(2 * at, 2)], ry.at[k, pl.ds(0, 2)], sy.at[k], ky.at[k], to_y(k))

    def gain_copy(k):
        return send(slim.at[pl.ds(2 * rows, 1)], ry.at[k, pl.ds(2, 1)], syg.at[k], kyg.at[k], to_y(k))

    @pl.loop(1, rows)
    def _(k):
        y_copy(k).start()
        gain_copy(k).start()

    mine[pl.ds(0, 2)] = slim[pl.ds(2 * y, 2)]
    mine[pl.ds(2, 1)] = slim[pl.ds(2 * rows, 1)]

    @pl.loop(1, rows)
    def _(k):
        y_copy(k).wait_recv()
        gain_copy(k).wait_recv()
        mine[...] += ry[k]

    half_copy = send(mine, rhi, shi, khi, to_half)
    half_copy.start()
    half_copy.wait()
    mine[...] += rhi[...]

    def gather_copy(k):
        return send(mine.at[pl.ds(0, 2)], full.at[pl.ds(2 * y, 2)], sg.at[k], kg.at[k], to_y(k))

    @pl.loop(1, rows)
    def _(k):
        gather_copy(k).start()

    def arrival(k):
        at = (y + rows - k) % rows
        return send(mine.at[pl.ds(0, 2)], full.at[pl.ds(2 * at, 2)], sg.at[k], kg.at[k], to_y(k))

    @pl.loop(1, rows)
    def _(k):
        at = (y + rows - k) % rows
        arrival(k).wait_recv()
        out[pl.ds(2 * at, 2)] = full[pl.ds(2 * at, 2)]

    out[pl.ds(2 * y, 2)] = mine[pl.ds(0, 2)]
    out[pl.ds(2 * rows, 1)] = mine[pl.ds(2, 1)]

    core_copy(0).wait_send()
    low_copy.wait_send()

    @pl.loop(1, depth)
    def _(k):
        core_copy(k).wait_send()
        z_copy(k).wait_send()

    @pl.loop(1, rows)
    def _(k):
        y_copy(k).wait_send()
        gain_copy(k).wait_send()
        gather_copy(k).wait_send()


def reduce_gradients(part, depth, rows):
    count = part.shape[3]
    dma = pltpu.SemaphoreType.DMA

    def f32(*shape):
        return pltpu.VMEM(shape + (8, HEAD), jnp.float32)

    return pl.pallas_call(
        functools.partial(reduce_kernel, depth, rows),
        out_shape=jax.ShapeDtypeStruct((count, 8, HEAD), jnp.float32),
        in_specs=[pl.BlockSpec(memory_space=pltpu.VMEM)],
        out_specs=pl.BlockSpec(memory_space=pltpu.VMEM),
        scratch_shapes=[
            f32(depth, 2, count), f32(depth, 2, count), f32(depth, 2, count), f32(2, count), f32(count),
            f32(count), f32(rows, 3), f32(3), f32(3), f32(count),
            dma((depth,)), dma((depth,)), dma((depth,)), dma((depth,)), dma, dma,
            dma((rows,)), dma((rows,)), dma((rows,)), dma((rows,)), dma, dma, dma((rows,)), dma((rows,)),
        ],
        compiler_params=pltpu.CompilerParams(collective_id=2, has_side_effects=True),
        name="reduce_gradients",
    )(part)


def per_device(depth, rows, query_in, key_in, value_in, grad_out, w_query, w_key, norm_gain):
    width_all = query_in.shape[2]
    grad_query, grad_key, grad_value, part = attention(
        query_in[0], key_in[0], value_in[0], grad_out[0], w_query, w_key, norm_gain.reshape(1, width_all), depth, rows)
    total = reduce_gradients(part, depth, rows)
    own = HEAD // 2
    pairs = total[:-1].reshape(own // 8, 2, 8, HEAD)
    gains = total[-1, 0].reshape(2, own)
    total_gain = jnp.where(lax.axis_index("dp") % 2 == 0, gains[0], gains[1])
    return (
        grad_query[None],
        grad_key[None],
        grad_value[None],
        pairs[:, 0].reshape(own, HEAD),
        pairs[:, 1].reshape(own, HEAD),
        total_gain,
    )


def solution(mesh):
    tokens = P("dp", "seq", None)
    body = functools.partial(per_device, mesh.shape["dp"] // 4, mesh.shape["seq"] // 2)
    return jax.shard_map(
        body,
        mesh=mesh,
        in_specs=(tokens, tokens, tokens, tokens, P(), P(), P()),
        out_specs=(tokens, tokens, tokens, P("dp", None), P("dp", None), P("dp")),
        check_vma=False,
    )
```

time: 208 us -> 212 us (1.019)
  Pallas kernels: 164 us -> 205 us
  matrix products: 21.1 us -> 0 us
  local copies, waits for them, and re-layouts: 16.9 us -> 3.87 us
  other arithmetic: 3.73 us -> 1.33 us
    pallas_call x2 -> x1, Pallas kernels: 107 us -> 148 us  [attention(): pl.pallas_call(functools.partial(attention_kernel, rows), out_shape=(grad...]
    dot_general x18 -> x0, matrix products: 21.1 us -> none  [the longest x1 2.87 us: per_device(): jnp.einsum('bshe,bhfe->bshf', value_h.astype(jnp.float32), later_state, p...]
    unnamed x56 -> x9, local copies, waits for them, and re-layouts: 12.3 us -> 2.39 us
where the time goes in v2:
time: 212 us; the launch traced here: 211 us
  Pallas kernels  205 us (97%)
  local copies, waits for them, and re-layouts  3.87 us (2%)
    pallas_call x1, Pallas kernels, attention(): pl.pallas_call(functools.partial(attention_kernel, rows), out_shape=(grad...  148 us
    pallas_call x1, Pallas kernels, reduce_gradients(): pl.pallas_call(functools.partial(reduce_kernel, depth, rows), out_shape=j...  57.3 us

profile of v2, /device:TPU:6, one launch (start us, length us, event | category | flops | bytes accessed | tf_op | source)
XLA Modules:
  0.0 211.0 jit_solution(13888617195706811111)
XLA Ops:
  0.6 147.8 %attention.1 = (bf16[128,2048]{1,0:T(8,128)(2,1)}, bf16[128,2048]{1,0:T(8,128)(2,1)}, bf16[128,2048]{1,0:T(8,128)(2,1)}, f32[2,8,2,17,8,128]{5,4,3,2,1,0:T(8,128)}) custom-call(bf16[128,2048]{1,0:T(8,128)(2,1)} %bitcast.18, bf16[128,2048]{1,0:T(8,128)(2,1)} %bitcast.19, bf16[128,2048]{1,0:T(8,128)(2,1)} %bitcast.20, bf16[128,2048]{1,0:T(8,128)(2,1)} %bitcast.21, ...), custom_call_target="tpu_custom_call" | custom-call | tf_op jit(solution)/shard_map/attention/pallas_call | solution.py:199
  148.5 0.0 copy-start.2
  148.5 0.0 copy-start.1
  148.5 0.0 copy-start
  148.5 57.3 %reduce_gradients.1 = f32[17,8,128]{2,1,0:T(8,128)} custom-call(f32[2,8,2,17,8,128]{5,4,3,2,1,0:T(8,128)} %get-tuple-element.13.part), custom_call_target="tpu_custom_call" | custom-call | tf_op jit(solution)/shard_map/reduce_gradients/pallas_call | solution.py:338
  205.8 1.3 fusion
  207.1 0.8 slice.20
  207.9 0.6 slice_bitcast_fusion
  208.6 0.0 copy-done.2
  208.6 0.8 copy.16
  209.4 0.0 copy-done.1
  209.4 0.8 copy.17
  210.2 0.0 copy-done
  210.2 0.8 copy.18
Async XLA Ops:
  148.5 60.1 %copy-start.2 = (bf16[128,2048]{1,0:T(8,128)(2,1)S(1)}, bf16[128,2048]{1,0:T(8,128)(2,1)}, u32[]{:S(2)}) copy-start(bf16[128,2048]{1,0:T(8,128)(2,1)} %get-tuple-element.10) | copy-start | bytes 1572868
  148.5 60.9 %copy-start.1 = (bf16[128,2048]{1,0:T(8,128)(2,1)S(1)}, bf16[128,2048]{1,0:T(8,128)(2,1)}, u32[]{:S(2)}) copy-start(bf16[128,2048]{1,0:T(8,128)(2,1)} %get-tuple-element.11) | copy-start | bytes 1572868
  148.5 61.7 %copy-start = (bf16[128,2048]{1,0:T(8,128)(2,1)S(1)}, bf16[128,2048]{1,0:T(8,128)(2,1)}, u32[]{:S(2)}) copy-start(bf16[128,2048]{1,0:T(8,128)(2,1)} %get-tuple-element.12) | copy-start | bytes 1572868

commit v3 on v2

v3 whole, which is shorter than its diff:
```python
import functools

import jax
import jax.numpy as jnp
from jax import lax
from jax.experimental import pallas as pl
from jax.experimental.pallas import tpu as pltpu
from jax.sharding import PartitionSpec as P

HEAD = 128
MESH = pl.DeviceIdType.MESH

norm_eps = 1e-05


def product(left, right, over):
    return lax.dot_general(left, right, ((over[:1], over[1:]), ((), ())), preferred_element_type=jnp.float32)


def two_terms(wide):
    high = wide.astype(jnp.bfloat16)
    return high, (wide - high.astype(jnp.float32)).astype(jnp.bfloat16)


def exchange(src, dst, send_sem, recv_sem, device):
    return pltpu.make_async_remote_copy(
        src_ref=src, dst_ref=dst, send_sem=send_sem, recv_sem=recv_sem, device_id=device, device_id_type=MESH)


def attention_kernel(depth, rows, query, key, value, cotangent, wq, wk, gain, grad_query, grad_key, grad_value, out,
                     local, peer, inbox, outbox, adjoint, peer_adj, inbox_adj, outbox_adj,
                     feat_k, slope_k, part_fk, part_v, parts, rcore, summed, rz, block, rlo, slim, rrow, mine, rhi, full,
                     sx, rx, sy, ry, sx2, rx2, sy2, ry2, score, kcore, sz, kz,
                     slo, klo, srow, krow, srowg, krowg, shi, khi, sg, kg):
    heads = local.shape[0]
    dp, seq = lax.axis_index("dp"), lax.axis_index("seq")
    y, half = seq // 2, seq % 2
    top = rows - 1
    z, low, core = dp // 4, (dp // 2) % 2, dp % 2

    def to_z(k):
        return (((z + k) % depth) * 4 + low * 2 + core, seq)

    def to_y(k):
        return (dp, ((y + k) % rows) * 2 + half)

    to_core = (z * 4 + low * 2 + (1 - core), seq)
    to_low = (z * 4 + (1 - low) * 2 + core, seq)
    partner = (dp, y * 2 + (1 - half))
    above, below = to_y(1), to_y(rows - 1)
    barrier = pltpu.get_barrier_semaphore()
    others = [to_core, to_low, partner]
    others += [to_z(k) for k in range(1, depth)] + [to_y(k) for k in range(1, rows)]
    for other in others:
        pl.semaphore_signal(barrier, inc=1, device_id=other, device_id_type=MESH)
    pl.semaphore_wait(barrier, len(others))

    def across(h):
        return exchange(local.at[h], peer.at[h], sx.at[h], rx.at[h], partner)

    def upward(h):
        return exchange(outbox.at[h], inbox.at[h], sy.at[h], ry.at[h], above)

    def across_adj(h):
        return exchange(adjoint.at[h], peer_adj.at[h], sx2.at[h], rx2.at[h], partner)

    def downward(h):
        return exchange(outbox_adj.at[h], inbox_adj.at[h], sy2.at[h], ry2.at[h], below)

    def columns(h):
        return pl.ds(pl.multiple_of(((h + 2 * z) % heads) * HEAD, HEAD), HEAD)

    tiles = HEAD // 16
    sent = (pl.ds(0, tiles + 1), pl.ds(0, tiles))

    def core_copy(which, h):
        return exchange(parts.at[which, 1 - core, h, sent[which]], rcore.at[which, h, sent[which]],
                        score.at[which, h], kcore.at[which, h], to_core)

    def z_copy(which, h):
        return exchange(summed.at[which, h, sent[which]], rz.at[which, h, sent[which]],
                        sz.at[which, h], kz.at[which, h], to_z(h // 2))

    def relay(which, h):
        core_copy(which, h).wait_recv()
        summed[which, h, sent[which]] = parts[which, core, h, sent[which]] + rcore[which, h, sent[which]]

        @pl.when(h >= 2)
        def _():
            z_copy(which, h).start()

    tokens = query.shape[0]
    position = lax.broadcasted_iota(jnp.int32, (tokens, tokens), 0)
    column = lax.broadcasted_iota(jnp.int32, (tokens, tokens), 1)
    causal = position >= column

    def put_sums(h, which, total):
        own = HEAD // 2
        for side in range(2):
            parts[which, side, h, pl.ds(0, tiles)] = total[side * own : (side + 1) * own].reshape(tiles, 8, HEAD)

    @pl.loop(0, heads)
    def _(h):
        at = columns(h)
        pre = product(key[:, at], wk[at, :], (1, 0))
        slope = jnp.exp(jnp.minimum(pre, 0.0))
        feat = jnp.where(pre > 0.0, pre + 1.0, slope).astype(jnp.bfloat16)
        slope_k[h] = slope
        feat_k[h] = feat
        local[h] = product(feat, value[:, at], (0, 0))

        @pl.when(h > 0)
        def _():
            across(h - 1).start()

    @pl.when(y == 0)
    def _():
        inbox[...] = jnp.zeros_like(inbox)

    @pl.when(y == top)
    def _():
        inbox_adj[...] = jnp.zeros_like(inbox_adj)

    across(heads - 1).start()
    is_second = jnp.where(half == 1, 1.0, 0.0).astype(jnp.float32)

    def forward(h):
        at = columns(h)
        fk, v = feat_k[h], value[:, at]
        q, wq_h = query[:, at], wq[at, :]
        pre = product(q, wq_h, (1, 0))
        slope = jnp.exp(jnp.minimum(pre, 0.0))
        fq = jnp.where(pre > 0.0, pre + 1.0, slope).astype(jnp.bfloat16)
        attn = jnp.where(causal, product(fq, fk, (1, 1)), 0.0).astype(jnp.bfloat16)
        inner = product(attn, v, (1, 0))
        across(h).wait_recv()

        @pl.when(y != 0)
        def _():
            upward(h).wait_recv()

        outbox[h] = inbox[h] + (local[h] + peer[h])
        state_high, state_low = two_terms(inbox[h] + is_second * peer[h])

        @pl.when(y != top)
        def _():
            upward(h).start()

        numerator = inner + (product(fq, state_high, (1, 0)) + product(fq, state_low, (1, 0)))
        inv_rms = lax.rsqrt(jnp.mean(numerator * numerator, axis=-1, keepdims=True) + norm_eps)
        normed = numerator * inv_rms
        grad = cotangent[:, at].astype(jnp.float32)
        grad_normed = grad * gain[:, at]
        grad_numer = inv_rms * (
            grad_normed - normed * jnp.mean(grad_normed * normed, axis=-1, keepdims=True))
        low_numer, rest = two_terms(grad_numer)
        adjoint[h] = product(fq, low_numer, (0, 0))
        mixed = jnp.where(causal, product(low_numer, v, (1, 1)), 0.0).astype(jnp.bfloat16)
        grad_fq = product(mixed, fk, (1, 0)) + (
            product(low_numer, state_high, (1, 1)) + (product(low_numer, state_low, (1, 1)) + product(rest, state_high, (1, 1))))
        across_adj(h).start()
        pre_grad = (grad_fq * slope).astype(jnp.bfloat16)
        grad_query[:, at] = product(pre_grad, wq_h, (1, 1)).astype(jnp.bfloat16)
        put_sums(h, 0, product(q, pre_grad, (0, 0)))
        gains = jnp.broadcast_to(jnp.sum(normed * grad, axis=0, keepdims=True), (8, HEAD))
        for side in range(2):
            parts[0, side, h, tiles] = gains
        part_fk[h] = product(mixed, fq, (0, 0))
        part_v[h] = product(attn, low_numer, (0, 0))
        core_copy(0, h).start()

    def backward(h):
        at = columns(h)
        across_adj(h).wait_recv()

        @pl.when(y != top)
        def _():
            downward(h).wait_recv()

        outbox_adj[h] = inbox_adj[h] + (adjoint[h] + peer_adj[h])
        state_high, state_low = two_terms(inbox_adj[h] + (1.0 - is_second) * peer_adj[h])

        @pl.when(y != 0)
        def _():
            downward(h).start()

        v, fk, wk_h = value[:, at], feat_k[h], wk[at, :]
        grad_fk = part_fk[h] + (product(v, state_high, (1, 1)) + product(v, state_low, (1, 1)))
        pre_grad = (grad_fk * slope_k[h]).astype(jnp.bfloat16)
        grad_v = part_v[h] + (product(fk, state_high, (1, 0)) + product(fk, state_low, (1, 0)))
        put_sums(h, 1, product(key[:, at], pre_grad, (0, 0)))
        grad_value[:, at] = grad_v.astype(jnp.bfloat16)
        grad_key[:, at] = product(pre_grad, wk_h, (1, 1)).astype(jnp.bfloat16)
        core_copy(1, h).start()

        @pl.when(h >= 1)
        def _():
            relay(1, h - 1)

    lag = 2 + 3 * (top - y)

    @pl.loop(0, heads + 2 + 3 * top)
    def _(step):
        @pl.when(step < heads)
        def _():
            forward(step)

        @pl.when(step >= 1)
        def _():
            @pl.when(step <= heads)
            def _():
                relay(0, step - 1)

        @pl.when(step >= lag)
        def _():
            @pl.when(step < lag + heads)
            def _():
                backward(step - lag)

    relay(1, heads - 1)

    for which in range(2):
        for side in range(2):
            block[side, sent[which], which] = summed[which, side, sent[which]]

        @pl.loop(2, heads)
        def _(h):
            z_copy(which, h).wait_recv()
            block[h % 2, sent[which], which] += rz[which, h, sent[which]]

    for side in range(2):
        block[side, tiles, 1] = jnp.zeros((8, HEAD), jnp.float32)
    low_copy = exchange(block.at[1 - low], rlo, slo, klo, to_low)
    low_copy.start()
    low_copy.wait_recv()
    slim[...] = block[low] + rlo[...]

    def row_copy(k):
        return exchange(slim.at[(y + k) % rows], rrow.at[k, pl.ds(0, 2)], srow.at[k], krow.at[k], to_y(k))

    def gain_copy(k):
        return exchange(slim.at[tiles, pl.ds(0, 1)], rrow.at[k, pl.ds(2, 1)], srowg.at[k], krowg.at[k], to_y(k))

    @pl.loop(1, rows)
    def _(k):
        row_copy(k).start()
        gain_copy(k).start()

    mine[pl.ds(0, 2)] = slim[y]
    mine[pl.ds(2, 1)] = slim[tiles, pl.ds(0, 1)]

    @pl.loop(1, rows)
    def _(k):
        row_copy(k).wait_recv()
        gain_copy(k).wait_recv()
        mine[...] += rrow[k]

    half_copy = exchange(mine, rhi, shi, khi, partner)
    half_copy.start()
    half_copy.wait()
    mine[...] += rhi[...]

    def gather_copy(k, at):
        return exchange(mine.at[pl.ds(0, 2)], full.at[at], sg.at[k], kg.at[k], to_y(k))

    @pl.loop(1, rows)
    def _(k):
        gather_copy(k, y).start()

    out[y] = mine[pl.ds(0, 2)]
    out[tiles, pl.ds(0, 1)] = mine[pl.ds(2, 1)]
    out[tiles, 1] = jnp.zeros((8, HEAD), jnp.float32)

    @pl.loop(1, rows)
    def _(k):
        at = (y + rows - k) % rows
        gather_copy(k, at).wait_recv()
        out[at] = full[at]

    low_copy.wait_send()

    @pl.loop(1, rows)
    def _(k):
        row_copy(k).wait_send()
        gain_copy(k).wait_send()
        gather_copy(k, y).wait_send()

    for which in range(2):
        @pl.loop(0, heads)
        def _(h):
            core_copy(which, h).wait_send()

            @pl.when(h >= 2)
            def _():
                z_copy(which, h).wait_send()

    @pl.loop(0, heads)
    def _(h):
        across(h).wait_send()
        across_adj(h).wait_send()

        @pl.when(y != top)
        def _():
            upward(h).wait_send()

        @pl.when(y != 0)
        def _():
            downward(h).wait_send()


def attention(query, key, value, cotangent, wq, wk, gain, depth, rows):
    heads = wq.shape[0] // HEAD
    tokens, width = query.shape
    tiles = HEAD // 16
    states = pltpu.VMEM((heads, HEAD, HEAD), jnp.float32)
    dma = pltpu.SemaphoreType.DMA((heads,))
    one, each = pltpu.SemaphoreType.DMA, pltpu.SemaphoreType.DMA((rows,))

    def f32(*shape):
        return pltpu.VMEM(shape + (8, HEAD), jnp.float32)

    vmem = pl.BlockSpec(memory_space=pltpu.VMEM)
    grads = jax.ShapeDtypeStruct((tokens, width), jnp.bfloat16)
    return pl.pallas_call(
        functools.partial(attention_kernel, depth, rows),
        out_shape=(grads, grads, grads,
                   jax.ShapeDtypeStruct((tiles + 1, 2, 8, HEAD), jnp.float32)),
        in_specs=[vmem] * 7,
        out_specs=(vmem,) * 4,
        scratch_shapes=[states] * 8
        + [pltpu.VMEM((heads, tokens, HEAD), jnp.bfloat16), pltpu.VMEM((heads, tokens, HEAD), jnp.float32)]
        + [pltpu.VMEM((heads, tokens, HEAD), jnp.float32)] * 2
        + [f32(2, 2, heads, tiles + 1), f32(2, heads, tiles + 1), f32(2, heads, tiles + 1), f32(2, heads, tiles + 1)]
        + [f32(2, tiles + 1, 2), f32(tiles + 1, 2), f32(tiles + 1, 2), f32(rows, 3), f32(3), f32(3), f32(rows, 2)]
        + [dma] * 8
        + [pltpu.SemaphoreType.DMA((2, heads))] * 4
        + [one, one, each, each, each, each, one, one, each, each],
        compiler_params=pltpu.CompilerParams(collective_id=0, has_side_effects=True),
        name="attention",
    )(query, key, value, cotangent, wq, wk, gain)


def per_device(depth, rows, query_in, key_in, value_in, grad_out, w_query, w_key, norm_gain):
    width_all = query_in.shape[2]
    grad_query, grad_key, grad_value, total = attention(
        query_in[0], key_in[0], value_in[0], grad_out[0], w_query, w_key, norm_gain.reshape(1, width_all), depth, rows)
    own = HEAD // 2
    pairs = total[:-1]
    gains = total[-1, 0, 0].reshape(2, own)
    total_gain = jnp.where(lax.axis_index("dp") % 2 == 0, gains[0], gains[1])
    return (
        grad_query[None],
        grad_key[None],
        grad_value[None],
        pairs[:, 0].reshape(own, HEAD),
        pairs[:, 1].reshape(own, HEAD),
        total_gain,
    )


def solution(mesh):
    tokens = P("dp", "seq", None)
    body = functools.partial(per_device, mesh.shape["dp"] // 4, mesh.shape["seq"] // 2)
    return jax.shard_map(
        body,
        mesh=mesh,
        in_specs=(tokens, tokens, tokens, tokens, P(), P(), P()),
        out_specs=(tokens, tokens, tokens, P("dp", None), P("dp", None), P("dp")),
        check_vma=False,
    )
```

time: 212 us -> 139 us (0.66)
  Pallas kernels: 205 us -> 131 us
    pallas_call x2 -> x1, Pallas kernels: 205 us -> 131 us  [attention(): pl.pallas_call(functools.partial(attention_kernel, depth, rows), out_shap...]
where the time goes in v3:
time: 139 us; the launch traced here: 138 us
  Pallas kernels  131 us (94%)
  local copies, waits for them, and re-layouts  5.37 us (4%)
    pallas_call x1, Pallas kernels, attention(): pl.pallas_call(functools.partial(attention_kernel, depth, rows), out_shap...  131 us
    unnamed x7, local copies, waits for them, and re-layouts  3.96 us

profile of v3, /device:TPU:6, one launch (start us, length us, event | category | flops | bytes accessed | tf_op | source)
XLA Modules:
  0.0 138.5 jit_solution(3663316429454762890)
XLA Ops:
  0.6 131.1 %attention.1 = (bf16[128,2048]{1,0:T(8,128)(2,1)}, bf16[128,2048]{1,0:T(8,128)(2,1)}, bf16[128,2048]{1,0:T(8,128)(2,1)}, f32[9,2,8,128]{3,2,1,0:T(8,128)}) custom-call(bf16[128,2048]{1,0:T(8,128)(2,1)} %bitcast.17, bf16[128,2048]{1,0:T(8,128)(2,1)} %bitcast.18, bf16[128,2048]{1,0:T(8,128)(2,1)} %bitcast.19, bf16[128,2048]{1,0:T(8,128)(2,1)} %bitcast.20, ...), custom_call_target="tpu_custom_call" | custom-call | tf_op jit(solution)/shard_map/attention/pallas_call | solution.py:324
  131.7 1.3 fusion
  133.1 1.4 %slice_bitcast_fusion = (f32[64,128]{1,0:T(8,128)}, f32[64,128]{1,0:T(8,128)}) fusion(f32[9,2,8,128]{3,2,1,0:T(8,128)} %get-tuple-element.13), kind=kLoop, calls=%fused_computation | loop fusion | bytes 131072 | tf_op jit(solution)/shard_map/reshape;squeeze | solution.py:356
  134.5 0.0 copy-start.1
  134.5 1.9 %copy.16 = bf16[1,128,2048]{2,1,0:T(8,128)(2,1)} copy(bf16[1,128,2048]{2,1,0:T(8,128)(2,1)} %bitcast.16) | data formatting | bytes 1048576
  136.4 0.0 copy-done.1
  136.4 0.0 copy-start
  136.4 0.8 copy.17
  137.2 0.4 copy-done
  137.7 0.8 copy.18
Async XLA Ops:
  134.5 1.9 %copy-start.1 = (bf16[128,2048]{1,0:T(8,128)(2,1)S(1)}, bf16[128,2048]{1,0:T(8,128)(2,1)}, u32[]{:S(2)}) copy-start(bf16[128,2048]{1,0:T(8,128)(2,1)} %get-tuple-element.11) | copy-start | bytes 1572868
  136.4 1.2 copy-start

commit v4 on v3

--- a/solution.py
+++ b/solution.py
@@ -193,23 +193,23 @@
         grad_key[:, at] = product(pre_grad, wk_h, (1, 1)).astype(jnp.bfloat16)
         core_copy(1, h).start()
 
-        @pl.when(h >= 1)
-        def _():
-            relay(1, h - 1)
-
-    lag = 2 + 3 * (top - y)
-
-    @pl.loop(0, heads + 2 + 3 * top)
+        @pl.when(h >= 2)
+        def _():
+            relay(1, h - 2)
+
+    lag = 3 + 6 * (top - y)
+
+    @pl.loop(0, heads + 3 + 6 * top)
     def _(step):
         @pl.when(step < heads)
         def _():
             forward(step)
 
-        @pl.when(step >= 1)
-        def _():
-            @pl.when(step <= heads)
+        @pl.when(step >= 3)
+        def _():
+            @pl.when(step < heads + 3)
             def _():
-                relay(0, step - 1)
+                relay(0, step - 3)
 
         @pl.when(step >= lag)
         def _():
@@ -217,6 +217,7 @@
             def _():
                 backward(step - lag)
 
+    relay(1, heads - 2)
     relay(1, heads - 1)
 
     for which in range(2):

time: 139 us -> 135 us (0.971)
  Pallas kernels: 131 us -> 128 us
    pallas_call x1, Pallas kernels: 131 us -> 128 us  [attention(): pl.pallas_call(functools.partial(attention_kernel, depth, rows), out_shap...]
where the time goes in v4:
time: 135 us
  Pallas kernels  128 us (95%)
  local copies, waits for them, and re-layouts  5.37 us (4%)
    pallas_call x1, Pallas kernels, attention(): pl.pallas_call(functools.partial(attention_kernel, depth, rows), out_shap...  128 us
    unnamed x7, local copies, waits for them, and re-layouts  3.96 us

profile of v4, /device:TPU:6, one launch (start us, length us, event | category | flops | bytes accessed | tf_op | source)
XLA Modules:
  0.0 135.0 jit_solution(6847220484074757157)
XLA Ops:
  0.6 127.7 %attention.1 = (bf16[128,2048]{1,0:T(8,128)(2,1)}, bf16[128,2048]{1,0:T(8,128)(2,1)}, bf16[128,2048]{1,0:T(8,128)(2,1)}, f32[9,2,8,128]{3,2,1,0:T(8,128)}) custom-call(bf16[128,2048]{1,0:T(8,128)(2,1)} %bitcast.17, bf16[128,2048]{1,0:T(8,128)(2,1)} %bitcast.18, bf16[128,2048]{1,0:T(8,128)(2,1)} %bitcast.19, bf16[128,2048]{1,0:T(8,128)(2,1)} %bitcast.20, ...), custom_call_target="tpu_custom_call" | custom-call | tf_op jit(solution)/shard_map/attention/pallas_call | solution.py:325
  128.3 1.3 fusion
  129.7 1.4 %slice_bitcast_fusion = (f32[64,128]{1,0:T(8,128)}, f32[64,128]{1,0:T(8,128)}) fusion(f32[9,2,8,128]{3,2,1,0:T(8,128)} %get-tuple-element.13), kind=kLoop, calls=%fused_computation | loop fusion | bytes 131072 | tf_op jit(solution)/shard_map/reshape;squeeze | solution.py:357
  131.1 0.0 copy-start.1
  131.1 1.9 %copy.16 = bf16[1,128,2048]{2,1,0:T(8,128)(2,1)} copy(bf16[1,128,2048]{2,1,0:T(8,128)(2,1)} %bitcast.16) | data formatting | bytes 1048576
  133.0 0.0 copy-done.1
  133.0 0.0 copy-start
  133.0 0.8 copy.17
  133.8 0.4 copy-done
  134.2 0.8 copy.18
Async XLA Ops:
  131.1 1.9 %copy-start.1 = (bf16[128,2048]{1,0:T(8,128)(2,1)S(1)}, bf16[128,2048]{1,0:T(8,128)(2,1)}, u32[]{:S(2)}) copy-start(bf16[128,2048]{1,0:T(8,128)(2,1)} %get-tuple-element.11) | copy-start | bytes 1572868
  133.0 1.2 copy-start

commit v5 on v4

--- a/solution.py
+++ b/solution.py
@@ -8,6 +8,7 @@
 from jax.sharding import PartitionSpec as P
 
 HEAD = 128
+PIECES = 4
 MESH = pl.DeviceIdType.MESH
 
 norm_eps = 1e-05
@@ -58,14 +59,20 @@
     def across(h):
         return exchange(local.at[h], peer.at[h], sx.at[h], rx.at[h], partner)
 
-    def upward(h):
-        return exchange(outbox.at[h], inbox.at[h], sy.at[h], ry.at[h], above)
+    def piece(p):
+        return pl.ds(p * (HEAD // PIECES), HEAD // PIECES)
+
+    def upward(h, p):
+        return exchange(outbox.at[h, piece(p)], inbox.at[h, piece(p)], sy.at[h, p], ry.at[h, p], above)
 
     def across_adj(h):
         return exchange(adjoint.at[h], peer_adj.at[h], sx2.at[h], rx2.at[h], partner)
 
-    def downward(h):
-        return exchange(outbox_adj.at[h], inbox_adj.at[h], sy2.at[h], ry2.at[h], below)
+    def downward(h, p):
+        return exchange(outbox_adj.at[h, piece(p)], inbox_adj.at[h, piece(p)], sy2.at[h, p], ry2.at[h, p], below)
+
+    def joined(terms):
+        return tuple(jnp.concatenate(parts_of, axis=0) for parts_of in zip(*terms))
 
     def columns(h):
         return pl.ds(pl.multiple_of(((h + 2 * z) % heads) * HEAD, HEAD), HEAD)
@@ -135,16 +142,21 @@
         inner = product(attn, v, (1, 0))
         across(h).wait_recv()
 
-        @pl.when(y != 0)
-        def _():
-            upward(h).wait_recv()
-
-        outbox[h] = inbox[h] + (local[h] + peer[h])
-        state_high, state_low = two_terms(inbox[h] + is_second * peer[h])
-
-        @pl.when(y != top)
-        def _():
-            upward(h).start()
+        terms = []
+        for p in range(PIECES):
+            @pl.when(y != 0)
+            def _():
+                upward(h, p).wait_recv()
+
+            some = piece(p)
+            outbox[h, some] = inbox[h, some] + (local[h, some] + peer[h, some])
+            terms.append(two_terms(inbox[h, some] + is_second * peer[h, some]))
+
+            @pl.when(y != top)
+            def _():
+                upward(h, p).start()
+
+        state_high, state_low = joined(terms)
 
         numerator = inner + (product(fq, state_high, (1, 0)) + product(fq, state_low, (1, 0)))
         inv_rms = lax.rsqrt(jnp.mean(numerator * numerator, axis=-1, keepdims=True) + norm_eps)
@@ -173,16 +185,21 @@
         at = columns(h)
         across_adj(h).wait_recv()
 
-        @pl.when(y != top)
-        def _():
-            downward(h).wait_recv()
-
-        outbox_adj[h] = inbox_adj[h] + (adjoint[h] + peer_adj[h])
-        state_high, state_low = two_terms(inbox_adj[h] + (1.0 - is_second) * peer_adj[h])
-
-        @pl.when(y != 0)
-        def _():
-            downward(h).start()
+        terms = []
+        for p in range(PIECES):
+            @pl.when(y != top)
+            def _():
+                downward(h, p).wait_recv()
+
+            some = piece(p)
+            outbox_adj[h, some] = inbox_adj[h, some] + (adjoint[h, some] + peer_adj[h, some])
+            terms.append(two_terms(inbox_adj[h, some] + (1.0 - is_second) * peer_adj[h, some]))
+
+            @pl.when(y != 0)
+            def _():
+                downward(h, p).start()
+
+        state_high, state_low = joined(terms)
 
         v, fk, wk_h = value[:, at], feat_k[h], wk[at, :]
         grad_fk = part_fk[h] + (product(v, state_high, (1, 1)) + product(v, state_low, (1, 1)))
@@ -300,13 +317,14 @@
         across(h).wait_send()
         across_adj(h).wait_send()
 
-        @pl.when(y != top)
-        def _():
-            upward(h).wait_send()
-
-        @pl.when(y != 0)
-        def _():
-            downward(h).wait_send()
+        for p in range(PIECES):
+            @pl.when(y != top)
+            def _():
+                upward(h, p).wait_send()
+
+            @pl.when(y != 0)
+            def _():
+                downward(h, p).wait_send()
 
 
 def attention(query, key, value, cotangent, wq, wk, gain, depth, rows):
@@ -314,7 +332,7 @@
     tokens, width = query.shape
     tiles = HEAD // 16
     states = pltpu.VMEM((heads, HEAD, HEAD), jnp.float32)
-    dma = pltpu.SemaphoreType.DMA((heads,))
+    dma, pieces = pltpu.SemaphoreType.DMA((heads,)), pltpu.SemaphoreType.DMA((heads, PIECES))
     one, each = pltpu.SemaphoreType.DMA, pltpu.SemaphoreType.DMA((rows,))
 
     def f32(*shape):
@@ -333,7 +351,7 @@
         + [pltpu.VMEM((heads, tokens, HEAD), jnp.float32)] * 2
         + [f32(2, 2, heads, tiles + 1), f32(2, heads, tiles + 1), f32(2, heads, tiles + 1), f32(2, heads, tiles + 1)]
         + [f32(2, tiles + 1, 2), f32(tiles + 1, 2), f32(tiles + 1, 2), f32(rows, 3), f32(3), f32(3), f32(rows, 2)]
-        + [dma] * 8
+        + [dma, dma, pieces, pieces] * 2
         + [pltpu.SemaphoreType.DMA((2, heads))] * 4
         + [one, one, each, each, each, each, one, one, each, each],
         compiler_params=pltpu.CompilerParams(collective_id=0, has_side_effects=True),

time: 135 us -> 132 us (0.978)
  Pallas kernels: 128 us -> 124 us
    pallas_call x1, Pallas kernels: 128 us -> 124 us  [attention(): pl.pallas_call(functools.partial(attention_kernel, depth, rows), out_shap...]
where the time goes in v5:
time: 132 us; the launch traced here: 131 us
  Pallas kernels  124 us (94%)
  local copies, waits for them, and re-layouts  5.37 us (4%)
  other arithmetic  1.34 us (1%)
    pallas_call x1, Pallas kernels, attention(): pl.pallas_call(functools.partial(attention_kernel, depth, rows), out_shap...  124 us
    unnamed x7, local copies, waits for them, and re-layouts  3.96 us

profile of v5, /device:TPU:6, one launch (start us, length us, event | category | flops | bytes accessed | tf_op | source)
XLA Modules:
  0.0 131.3 jit_solution(10863579863623639712)
XLA Ops:
  0.6 124.0 %attention.1 = (bf16[128,2048]{1,0:T(8,128)(2,1)}, bf16[128,2048]{1,0:T(8,128)(2,1)}, bf16[128,2048]{1,0:T(8,128)(2,1)}, f32[9,2,8,128]{3,2,1,0:T(8,128)}) custom-call(bf16[128,2048]{1,0:T(8,128)(2,1)} %bitcast.17, bf16[128,2048]{1,0:T(8,128)(2,1)} %bitcast.18, bf16[128,2048]{1,0:T(8,128)(2,1)} %bitcast.19, bf16[128,2048]{1,0:T(8,128)(2,1)} %bitcast.20, ...), custom_call_target="tpu_custom_call" | custom-call | tf_op jit(solution)/shard_map/attention/pallas_call | solution.py:343
  124.6 1.3 %fusion = f32[64]{0:T(128)} fusion(pred[]{:T(512)S(6)} %eq.5, f32[9,2,8,128]{3,2,1,0:T(8,128)} %get-tuple-element.13), kind=kLoop, calls=%fused_computation.3 | loop fusion | flops 64 | bytes 769 | tf_op jit(solution)/shard_map/jit(_where)/select_n | solution.py:369
  126.0 1.4 %slice_bitcast_fusion = (f32[64,128]{1,0:T(8,128)}, f32[64,128]{1,0:T(8,128)}) fusion(f32[9,2,8,128]{3,2,1,0:T(8,128)} %get-tuple-element.13), kind=kLoop, calls=%fused_computation | loop fusion | bytes 131072 | tf_op jit(solution)/shard_map/reshape;squeeze | solution.py:375
  127.4 0.0 copy-start.1
  127.4 1.9 %copy.16 = bf16[1,128,2048]{2,1,0:T(8,128)(2,1)} copy(bf16[1,128,2048]{2,1,0:T(8,128)(2,1)} %bitcast.16) | data formatting | bytes 1048576
  129.3 0.0 copy-done.1
  129.3 0.0 copy-start
  129.3 0.8 copy.17
  130.1 0.4 copy-done
  130.5 0.8 copy.18
Async XLA Ops:
  127.4 1.9 %copy-start.1 = (bf16[128,2048]{1,0:T(8,128)(2,1)S(1)}, bf16[128,2048]{1,0:T(8,128)(2,1)}, u32[]{:S(2)}) copy-start(bf16[128,2048]{1,0:T(8,128)(2,1)} %get-tuple-element.11) | copy-start | bytes 1572868
  129.3 1.2 copy-start

commit v6 on v5

--- a/solution.py
+++ b/solution.py
@@ -28,7 +28,7 @@
         src_ref=src, dst_ref=dst, send_sem=send_sem, recv_sem=recv_sem, device_id=device, device_id_type=MESH)
 
 
-def attention_kernel(depth, rows, query, key, value, cotangent, wq, wk, gain, grad_query, grad_key, grad_value, out,
+def attention_kernel(depth, rows, query, key, value, cotangent, wq, wk, gain, grad_query, grad_key, grad_value, out_wq, out_wk, out_gain,
                      local, peer, inbox, outbox, adjoint, peer_adj, inbox_adj, outbox_adj,
                      feat_k, slope_k, part_fk, part_v, parts, rcore, summed, rz, block, rlo, slim, rrow, mine, rhi, full,
                      sx, rx, sy, ry, sx2, rx2, sy2, ry2, score, kcore, sz, kz,
@@ -285,15 +285,18 @@
     def _(k):
         gather_copy(k, y).start()
 
-    out[y] = mine[pl.ds(0, 2)]
-    out[tiles, pl.ds(0, 1)] = mine[pl.ds(2, 1)]
-    out[tiles, 1] = jnp.zeros((8, HEAD), jnp.float32)
+    out_wq[y] = mine[0]
+    out_wk[y] = mine[1]
+    first_core = jnp.where(core == 0, 1.0, 0.0).astype(jnp.float32)
+    gains = mine[2]
+    out_gain[...] = first_core * gains[:1, : HEAD // 2] + (1.0 - first_core) * gains[:1, HEAD // 2 :]
 
     @pl.loop(1, rows)
     def _(k):
         at = (y + rows - k) % rows
         gather_copy(k, at).wait_recv()
-        out[at] = full[at]
+        out_wq[at] = full[at, 0]
+        out_wk[at] = full[at, 1]
 
     low_copy.wait_send()
 
@@ -343,9 +346,11 @@
     return pl.pallas_call(
         functools.partial(attention_kernel, depth, rows),
         out_shape=(grads, grads, grads,
-                   jax.ShapeDtypeStruct((tiles + 1, 2, 8, HEAD), jnp.float32)),
+                   jax.ShapeDtypeStruct((tiles, 8, HEAD), jnp.float32),
+                   jax.ShapeDtypeStruct((tiles, 8, HEAD), jnp.float32),
+                   jax.ShapeDtypeStruct((1, HEAD // 2), jnp.float32)),
         in_specs=[vmem] * 7,
-        out_specs=(vmem,) * 4,
+        out_specs=(vmem,) * 6,
         scratch_shapes=[states] * 8
         + [pltpu.VMEM((heads, tokens, HEAD), jnp.bfloat16), pltpu.VMEM((heads, tokens, HEAD), jnp.float32)]
         + [pltpu.VMEM((heads, tokens, HEAD), jnp.float32)] * 2
@@ -361,19 +366,16 @@
 
 def per_device(depth, rows, query_in, key_in, value_in, grad_out, w_query, w_key, norm_gain):
     width_all = query_in.shape[2]
-    grad_query, grad_key, grad_value, total = attention(
+    grad_query, grad_key, grad_value, total_wq, total_wk, total_gain = attention(
         query_in[0], key_in[0], value_in[0], grad_out[0], w_query, w_key, norm_gain.reshape(1, width_all), depth, rows)
     own = HEAD // 2
-    pairs = total[:-1]
-    gains = total[-1, 0, 0].reshape(2, own)
-    total_gain = jnp.where(lax.axis_index("dp") % 2 == 0, gains[0], gains[1])
     return (
         grad_query[None],
         grad_key[None],
         grad_value[None],
-        pairs[:, 0].reshape(own, HEAD),
-        pairs[:, 1].reshape(own, HEAD),
-        total_gain,
+        total_wq.reshape(own, HEAD),
+        total_wk.reshape(own, HEAD),
+        total_gain.reshape(own),
     )
 
 

time: 132 us -> 131 us (level)
  other arithmetic: 1.34 us -> 0 us
    unnamed x7 -> x16, local copies, waits for them, and re-layouts: 3.96 us -> 5.91 us
    another operation x1 -> x0, local copies, waits for them, and re-layouts: 1.4 us -> none  [per_device(): pairs[:, 1].reshape(own, HEAD)]
    select_n x1 -> x0, other arithmetic: 1.34 us -> none  [per_device(): total_gain = jnp.where(lax.axis_index('dp') % 2 == 0, gains[0], gains[1])]
where the time goes in v6:
time: 131 us
  Pallas kernels  124 us (95%)
  local copies, waits for them, and re-layouts  5.91 us (5%)
    pallas_call x1, Pallas kernels, attention(): pl.pallas_call(functools.partial(attention_kernel, depth, rows), out_shap...  124 us
    unnamed x16, local copies, waits for them, and re-layouts  5.91 us

profile of v6, /device:TPU:6, one launch (start us, length us, event | category | flops | bytes accessed | tf_op | source)
XLA Modules:
  0.0 130.5 jit_solution(2533664171167524661)
XLA Ops:
  0.6 123.9 %attention.1 = (bf16[128,2048]{1,0:T(8,128)(2,1)}, bf16[128,2048]{1,0:T(8,128)(2,1)}, bf16[128,2048]{1,0:T(8,128)(2,1)}, f32[8,8,128]{2,1,0:T(8,128)}, f32[8,8,128]{2,1,0:T(8,128)}, /*index=5*/f32[1,64]{1,0:T(1,128)}) custom-call(bf16[128,2048]{1,0:T(8,128)(2,1)} %bitcast.14, bf16[128,2048]{1,0:T(8,128)(2,1)} %bitcast.15, bf16[128,2048]{1,0:T(8,128)(2,1)} %bitcast.16, ...), custom_call_target="tpu_custom_call" | custom-call | tf_op jit(solution)/shard_map/attention/pallas_call | solution.py:346
  124.6 0.0 copy-start.1
  124.6 1.9 %copy.19 = bf16[1,128,2048]{2,1,0:T(8,128)(2,1)} copy(bf16[1,128,2048]{2,1,0:T(8,128)(2,1)} %bitcast.13) | data formatting | bytes 1048576
  126.5 0.0 copy-done.1
  126.5 0.0 copy-start
  126.5 0.8 copy.20
  127.3 0.4 copy-done
  127.8 0.0 copy-start.3
  127.8 0.8 copy.21
  128.6 0.0 copy-done.3
  128.6 0.0 copy-start.2
  128.6 0.6 copy.22
  129.2 0.2 copy-done.2
  129.3 0.0 copy-start.4
  129.3 0.6 copy.23
  130.0 0.0 copy-done.4
  130.0 0.5 copy.24
Async XLA Ops:
  124.6 2.0 %copy-start.1 = (bf16[128,2048]{1,0:T(8,128)(2,1)S(1)}, bf16[128,2048]{1,0:T(8,128)(2,1)}, u32[]{:S(2)}) copy-start(bf16[128,2048]{1,0:T(8,128)(2,1)} %get-tuple-element.13) | copy-start | bytes 1572868
  126.5 1.2 copy-start
  127.8 0.8 copy-start.3
  128.6 0.8 copy-start.2
  129.3 0.7 copy-start.4
